TPU v7x, 256 devices: a whole 4x4x8 slice. The times are simulated.
256 devices in a mesh: seq: 16 (over z, core), head: 16 (over x, y).
Axes of the slice: x: 4, y: 4, z: 8, core: 2. Of those that a mesh axis runs over, the one named last changes fastest.
Arguments:
- queries: bfloat16 [4096, 16384], P('seq', 'head'), may hold values from -8 to 8
- keys: bfloat16 [4096, 1024], P('seq'), may hold values from -8 to 8
- values: bfloat16 [4096, 1024], P('seq'), may hold values from -8 to 8
- query_map: bfloat16 [128, 128, 128], P('head'), may hold values from -3 to 3
- key_map: bfloat16 [8, 128, 128], replicated, may hold values from -3 to 3
- positions: int32 [4096], P('seq'), may hold values from 0 to 131071, as said below
Outputs:
- error_grad: bfloat16 [4096, 16384], P('seq', 'head')
Inputs may be any that keep to these rules, and one draw needn't show every extreme that they name: `positions`: each token's position is one more than the token before it, or 0 where a new document begins; the window begins inside a document that ends at position 131071, and at least one document begins inside the window.
All inputs are finite; a program needn't handle non-finite values.
Results may differ from a plain program's by a relative error of at most 0.0085.
Values may be sent and summed in bfloat16 or wider, within the bound.
No kernel may reach another device: no remote copies, remote signals or barrier semaphores. Data moves between devices by JAX's collectives and lax.ppermute only.
A program may use at most 64 MiB of HBM per device.

v0:
```python
from functools import partial
import math

import jax
import jax.numpy as jnp
from jax import lax
from jax.sharding import Mesh
from jax.sharding import PartitionSpec as P

QHEADS = 128
KVH = 8
LENGTH = 131072
SEQ = ("seq_0", "seq_1")


epsilon = 1e-06
masked_score = -1e30
highest = lax.Precision.HIGHEST


def in_one_piece(arrays, axis, dim, along):
    both = jnp.concatenate(arrays, axis=along)
    out, at, finished = (lax.all_gather(both, axis, axis=dim, tiled=True), 0, [])
    for a in arrays:
        finished.append(lax.slice_in_dim(out, at, at + a.shape[along], axis=along))
        at += a.shape[along]
    return tuple(finished)


def filled_with(x, identity):
    return jax.tree.map(
        lambda a, e: jnp.broadcast_to(jnp.asarray(e, a.dtype), a.shape), x, identity
    )


def prefix_by_axis(x, axes, combine, identity):
    before = start = filled_with(x, identity)
    total = x
    for axis in reversed(axes):
        devices, index = (lax.axis_size(axis), lax.axis_index(axis))
        pieces = jax.tree.map(
            lambda part, kind: lax.all_gather(part.astype(kind), axis),
            total,
            (jnp.bfloat16, jnp.bfloat16),
        )
        inside, total = (start, start)
        for k in range(devices):
            passed = k < index
            total = combine(
                total, jax.tree.map(lambda part, own: part[k].astype(own.dtype), pieces, x)
            )
            inside = jax.tree.map(lambda new, old: jnp.where(passed, new, old), total, inside)
        before = combine(inside, before)
    return before


def feature_map(inputs, weights, cosine_part, sine_part):
    projected = jnp.einsum("thd,hde->hte", inputs, weights, preferred_element_type=jnp.float32)
    mapped = jax.nn.elu(projected) + 1.0
    return jnp.concatenate([cosine_part * mapped, sine_part * mapped], axis=2).astype(jnp.bfloat16)


def add_pair(before_part, after_part):
    return (before_part[0] + after_part[0], before_part[1] + after_part[1])


def keep_state(status):
    return status


def attend(status, query_block, query_place, key_block, value_block, key_place, scaling):
    running, weight_sum, weighted = status
    scores = (
        jnp.einsum("qgpd,kgd->gpqk", query_block, key_block, preferred_element_type=jnp.float32)
        * scaling
    )
    visible = query_place[:, None] >= key_place[None, :]
    scores = jnp.where(visible, scores, masked_score)
    largest = jnp.maximum(running, jnp.max(scores, axis=-1))
    weights = jnp.where(visible, jnp.exp(scores - largest[..., None]), 0.0)
    factor = jnp.exp(running - largest)
    weight_sum = weight_sum * factor + jnp.sum(weights, axis=-1)
    weighted = weighted * factor[..., None] + jnp.einsum(
        "gpqk,kgd->gpqd",
        weights.astype(jnp.bfloat16),
        value_block,
        preferred_element_type=jnp.float32,
    )
    return (largest, weight_sum, weighted)


def per_device(queries, keys, values, query_map, key_map, positions):
    tokens = queries.shape[0]
    head_dim = key_map.shape[1]
    local_heads = query_map.shape[0]
    group_size = QHEADS // KVH
    kv_local = max(1, local_heads // group_size)
    per_group = local_heads // kv_local
    device = lax.axis_index(SEQ)
    first_group = lax.axis_index("head") * local_heads // group_size
    keys_mine = lax.dynamic_slice_in_dim(keys, first_group * head_dim, kv_local * head_dim, 1)
    values_mine = lax.dynamic_slice_in_dim(values, first_group * head_dim, kv_local * head_dim, 1)
    width_query = queries.shape[1]
    teacher_queries, teacher_keys, teacher_values = (queries, keys_mine, values_mine)
    query_place = device * tokens + jnp.arange(tokens, dtype=jnp.int32)
    grouped = teacher_queries.reshape(tokens, kv_local, per_group, head_dim)
    scaling = 1.0 / math.sqrt(head_dim)
    start_state = (
        jnp.full((kv_local, per_group, tokens), masked_score, jnp.float32),
        jnp.zeros((kv_local, per_group, tokens), jnp.float32),
        jnp.zeros((kv_local, per_group, tokens, head_dim), jnp.float32),
    )
    running_state = start_state
    piece_keys, piece_values = in_one_piece((teacher_keys, teacher_values), SEQ, 0, 1)
    row_count = piece_keys.shape[0]
    block_keys = math.gcd(row_count, 1024)
    blocks = row_count // block_keys
    key_place = jnp.arange(row_count, dtype=jnp.int32).reshape(blocks, block_keys)
    key_blocks = piece_keys.reshape(blocks, block_keys, kv_local, head_dim)
    value_blocks = piece_values.reshape(blocks, block_keys, kv_local, head_dim)

    def advance(status, inputs):
        key_block, value_block, key_row = inputs
        beyond = jnp.min(key_row) > jnp.max(query_place)
        compute_block = partial(
            attend,
            query_block=grouped,
            query_place=query_place,
            key_block=key_block,
            value_block=value_block,
            key_place=key_row,
            scaling=scaling,
        )
        return (lax.cond(beyond, keep_state, compute_block, status), None)

    running_state, unused = lax.scan(advance, running_state, (key_blocks, value_blocks, key_place))
    running, weight_sum, weighted = running_state
    result = weighted / weight_sum[..., None]
    teacher_out = (
        jnp.transpose(result, (2, 0, 1, 3)).reshape(tokens, width_query).astype(jnp.bfloat16)
    )
    angles = 0.5 * math.pi / LENGTH * positions.astype(jnp.float32)
    cosine_part = jnp.cos(angles)[None, :, None]
    sine_part = jnp.sin(angles)[None, :, None]
    query_feats = feature_map(
        queries.reshape(tokens, local_heads, head_dim), query_map, cosine_part, sine_part
    )
    map_mine = lax.dynamic_slice_in_dim(key_map, first_group, kv_local, 0)
    values_grouped = values_mine.reshape(tokens, kv_local, head_dim)
    key_feats = feature_map(
        keys_mine.reshape(tokens, kv_local, head_dim), map_mine, cosine_part, sine_part
    )
    totals = jnp.einsum(
        "gtf,tgd->gfd", key_feats, values_grouped, preferred_element_type=jnp.float32
    )
    masses = jnp.sum(key_feats, axis=1, dtype=jnp.float32)
    before, mass_before = prefix_by_axis(
        (totals, masses), SEQ, add_pair, (jnp.zeros_like(totals), jnp.zeros_like(masses))
    )
    feats_grouped = query_feats.reshape(kv_local, per_group, tokens, 2 * head_dim)
    causal = jnp.arange(tokens)[:, None] >= jnp.arange(tokens)[None, :]
    inner_block = jnp.where(
        causal,
        jnp.einsum("gptf,gsf->gpts", feats_grouped, key_feats, preferred_element_type=jnp.float32),
        0.0,
    )
    feats_wide = feats_grouped.astype(jnp.float32)
    values_wide = values_grouped.astype(jnp.float32)
    numerator = jnp.einsum(
        "gpts,sgd->gptd", inner_block, values_wide, precision=highest
    ) + jnp.einsum("gptf,gfd->gptd", feats_wide, before, precision=highest)
    denominator = jnp.sum(inner_block, axis=-1) + jnp.einsum(
        "gptf,gf->gpt", feats_wide, mass_before, precision=highest
    )
    student = numerator / (denominator[..., None] + epsilon)
    student = jnp.transpose(student, (2, 0, 1, 3)).reshape(tokens, width_query)
    return (2.0 * (student - teacher_out.astype(jnp.float32))).astype(jnp.bfloat16)


def solution(mesh):
    split = Mesh(mesh.devices.reshape(8, 2, mesh.shape["head"]), ("seq_0", "seq_1", "head"))
    placed = (P(SEQ, "head"), P(SEQ, None), P(SEQ, None), P("head", None, None), P(), P(SEQ))
    return jax.shard_map(
        per_device, mesh=split, in_specs=placed, out_specs=P(SEQ, "head"), check_vma=False
    )
```

profile of v0, /device:TPU:208, one launch (start us, length us, event | category | flops | bytes accessed | tf_op | source)
XLA Modules:
  0.0 118.4 jit_solution(2266864343722325257)
XLA Ops:
  6.5 1.0 copy-done
  7.7 0.9 constant_dynamic-slice_fusion.1
  8.7 0.7 pad_maximum_fusion.5
  9.4 0.7 add_reduce_fusion
  10.1 1.2 %copy.56 = bf16[256,1024]{0,1:T(8,128)(2,1)S(1)} copy(bf16[256,1024]{1,0:T(8,128)(2,1)} %param.10) | data formatting | bytes 1048576 | tf_op args[0]
  11.3 0.3 copy.58
  11.6 0.7 fusion.117
  12.3 1.0 multiply_convert_fusion.3
  13.5 0.2 convolution_convert_fusion
  13.7 1.9 %all-gather = bf16[512,128]{0,1:T(8,128)(2,1)S(1)} all-gather(bf16[256,128]{0,1:T(8,128)(2,1)S(1)} %convolution_convert_fusion), channel_id=2, replica_groups=mesh['seq_0'=8,'seq_1'=2,'head'=16] {'seq_1'}, dimensions={0}, use_global_device_ids=true | all-gather | bytes 196608 | tf_op jit(solution)/shard_map/all_gather | solution.py:42
  15.7 25.0 %all_gather.25 = bf16[8,1,256,128]{3,2,1,0:T(8,128)(2,1)S(1)} all-gather(bf16[1,1,256,128]{3,2,1,0:T(8,128)(2,1)S(1)} %copy.46), channel_id=1, replica_groups=mesh['seq_0'=8,'seq_1'=2,'head'=16] {'seq_0'}, dimensions={0}, use_global_device_ids=true | all-gather | bytes 589824 | tf_op jit(solution)/shard_map/all_gather | solution.py:42
  41.6 1.8 %all-gather.2 = bf16[2,1,256]{2,1,0:T(2,128)(2,1)S(1)} all-gather(bf16[1,1,256]{2,1,0:T(2,128)(2,1)S(1)} %reshape.451), channel_id=3, replica_groups=mesh['seq_0'=8,'seq_1'=2,'head'=16] {'seq_1'}, dimensions={0}, use_global_device_ids=true | all-gather | bytes 1536 | tf_op jit(solution)/shard_map/all_gather | solution.py:42
  43.5 14.5 %all_gather.28 = bf16[8,1,256]{2,1,0:T(2,128)(2,1)S(1)} all-gather(bf16[1,1,256]{2,1,0:T(2,128)(2,1)S(1)} %fusion.127), channel_id=1, replica_groups=mesh['seq_0'=8,'seq_1'=2,'head'=16] {'seq_0'}, dimensions={0}, use_global_device_ids=true | all-gather | bytes 4608 | tf_op jit(solution)/shard_map/all_gather | solution.py:42
  58.0 1.8 %multiply_convert_fusion.1 = (bf16[8,256,128]{1,2,0:T(8,128)(2,1)S(1)}, bf16[8,256,128]{1,2,0:T(8,128)(2,1)S(1)}) fusion(f32[256]{0:T(256)S(1)} %get-tuple-element.279, f32[256]{0:T(256)S(1)} %get-tuple-element.280, bf16[8,128,128]{2,1,0:T(8,128)(2,1)} %param.13, bf16[256,1024]{1,0:T(8,128)(2,1)} %param.10), kind=kOutput, calls=%fused_computation.47 | convolution fusion | flops 69206016 | bytes 1837056 | tf_op jit(solution)/shard_map/thd,hde->hte/dot_general | solution.py:58
  59.8 0.5 fusion.54
  60.3 1.9 %select_reduce_fusion = (f32[8,256]{1,0:T(8,128)S(1)}, f32[8,256,256]{1,2,0:T(8,128)}) fusion(pred[256,256]{0,1:T(8,128)(4,1)S(1)} %iota_compare_fusion, bf16[256,128]{0,1:T(8,128)(2,1)S(1)} %get-tuple-element.278, bf16[256,128]{0,1:T(8,128)(2,1)S(1)} %get-tuple-element.277, bf16[8,256,128]{1,2,0:T(8,128)(2,1)S(1)} %get-tuple-element.268, ...), kind=kOutput, calls=%fused_computation.31 | convolution fusion | flops 271841280 | bytes 3350528 | tf_op jit(solution)/shard_map/gptf,gsf->gpts/dot_general | solution.py:164
  62.2 1.7 %fusion.55 = f32[8,256,128]{1,2,0:T(8,128)} fusion(bf16[8,256,128]{1,2,0:T(8,128)(2,1)S(1)} %get-tuple-element.268, bf16[8,256,128]{1,2,0:T(8,128)(2,1)S(1)} %get-tuple-element.267, bf16[1,1,256,128]{2,3,1,0:T(8,128)(2,1)S(1)} %copy.75, bf16[1,1,256,128]{2,3,1,0:T(8,128)(2,1)S(1)} %copy.82, bf16[1,1,256,128]{2,3,1,0:T(8,128)(2,1)S(1)} %copy.81, ...), kind=kOutput, calls=%fused_computation.55 | convolution fusion | flops 808353792 | bytes 2752522 | tf_op jit(solution)/shard_map/gptf,gfd->gptd/dot_general | solution.py:171
  63.9 2.7 %fusion.130 = (bf16[4096,128]{0,1:T(8,128)(2,1)S(1)}, bf16[4096,128]{0,1:T(8,128)(2,1)}) fusion(bf16[4096,256]{0,1:T(8,128)(2,1)} %all-gather.5.cloned.1.call-done), kind=kLoop, calls=%fused_computation.162 | loop fusion | bytes 4194304 | tf_op jit(solution)/shard_map/slice | solution.py:25
  66.6 1.6 %copy.71 = bf16[4096,128]{1,0:T(8,128)(2,1)S(1)} copy(bf16[4096,128]{0,1:T(8,128)(2,1)} %get-tuple-element.266) | data formatting | bytes 2097152
  68.2 1.3 %copy.72 = bf16[4096,128]{1,0:T(8,128)(2,1)} copy(bf16[4096,128]{0,1:T(8,128)(2,1)S(1)} %get-tuple-element.265) | data formatting | bytes 2097152
  69.7 37.5 %while.16 = (s32[]{:T(128)}, f32[1,8,256]{2,1,0:T(8,128)S(1)}, f32[1,8,256]{2,1,0:T(8,128)S(1)}, f32[1,8,256,128]{3,2,1,0:T(8,128)S(1)}, s32[4,1024]{1,0:T(4,128...) while((s32[]{:T(128)}, f32[1,8,256]{2,1,0:T(8,128)S(1)}, ...), condition=%wide.region_9.10_spmd.clone, body=%wide.region_3.9_spmd.clone.sunk | while | flops 1101798656 | bytes 29508364 | solution.py:136
  69.7 0.6 fusion.137
  71.6 7.4 %conditional.3 = (f32[1,8,256]{2,1,0:T(8,128)S(1)}, f32[1,8,256]{2,1,0:T(8,128)S(1)}, f32[1,8,256,128]{3,2,1,0:T(8,128)S(1)}) conditional(s32[]{:T(128)} %convert_element_type.451, (s32[]{:T(128)}, s32[1,1024]{1,0:T(1,128)S(1)}, bf16[4,1024,1,128]{3,1,2,0:T(8,128)(2,1)S(1)}, s32[]{:T(128)}, bf16[256,1,8,128]{3,0,2,1:T(8,128)(2,1)S(1)}, ...), branch_computations={%region_5.7_spmd, %region_8.8_spmd} | conditional | flops 1101797632 | bytes 29482528 | solution.py:134
  71.6 0.2 broadcast_compare_fusion
  71.8 1.4 %fusion.2 = (f32[8,256]{1,0:T(8,128)S(1)}, f32[1024,256,8]{1,0,2:T(8,128)S(1)}) fusion(pred[256,1024]{0,1:T(8,128)(4,1)S(1)} %broadcast_compare_fusion, bf16[256,1,8,128]{3,0,2,1:T(8,128)(2,1)S(1)} %get-tuple-element.158, bf16[4,1024,1,128]{3,1,2,0:T(8,128)(2,1)S(1)} %get-tuple-element.156, s32[]{:T(128)} %get-tuple-element.157), kind=kOutput, calls=%fused_computation.3 | convolution fusion | flops 543160320 | bytes 9445380 | tf_op jit(solution)/shard_map/while/body/eval_jaxpr/cond/branch_0_fun/qgpd,kgd->gpqk/dot_general | solution.py:74
  73.3 2.0 %fusion.4 = f32[8,256]{1,0:T(8,128)S(1)} fusion(f32[1024,256,8]{1,0,2:T(8,128)S(1)} %get-tuple-element.264, f32[8,256]{1,0:T(8,128)S(1)} %bitcast.121, pred[256,1024]{0,1:T(8,128)(4,1)S(1)} %broadcast_compare_fusion), kind=kLoop, calls=%fused_computation.5 | loop fusion | flops 10483712 | bytes 8667136 | tf_op jit(solution)/shard_map/while/body/eval_jaxpr/cond/branch_0_fun/reduce_sum | solution.py:82
  75.3 3.7 %fusion.12 = f32[1,8,256,128]{3,2,1,0:T(8,128)S(1)} fusion(f32[1024,256,8]{1,0,2:T(8,128)S(1)} %get-tuple-element.264, f32[8,256]{1,0:T(8,128)S(1)} %bitcast.122, pred[256,1024]{0,1:T(8,128)(4,1)S(1)} %broadcast_compare_fusion, f32[1,8,256,128]{3,2,1,0:T(8,128)S(1)} %get-tuple-element.160, f32[8,256]{1,0:T(8,128)S(1)} %get-tuple-element.259, ...), kind=kOutput, calls=%fused_computation.10 | convolution fusion | flops 547880960 | bytes 11026944 | tf_op jit(solution)/shard_map/while/body/eval_jaxpr/cond/branch_0_fun/gpqk,kgd->gpqd/dot_general | solution.py:83
  79.0 0.6 fusion.137
  81.0 7.4 %conditional.3 = (f32[1,8,256]{2,1,0:T(8,128)S(1)}, f32[1,8,256]{2,1,0:T(8,128)S(1)}, f32[1,8,256,128]{3,2,1,0:T(8,128)S(1)}) conditional(s32[]{:T(128)} %convert_element_type.451, (s32[]{:T(128)}, s32[1,1024]{1,0:T(1,128)S(1)}, bf16[4,1024,1,128]{3,1,2,0:T(8,128)(2,1)S(1)}, s32[]{:T(128)}, bf16[256,1,8,128]{3,0,2,1:T(8,128)(2,1)S(1)}, ...), branch_computations={%region_5.7_spmd, %region_8.8_spmd} | conditional | flops 1101797632 | bytes 29482528 | solution.py:134
  81.0 0.2 broadcast_compare_fusion
  81.2 1.4 %fusion.2 = (f32[8,256]{1,0:T(8,128)S(1)}, f32[1024,256,8]{1,0,2:T(8,128)S(1)}) fusion(pred[256,1024]{0,1:T(8,128)(4,1)S(1)} %broadcast_compare_fusion, bf16[256,1,8,128]{3,0,2,1:T(8,128)(2,1)S(1)} %get-tuple-element.158, bf16[4,1024,1,128]{3,1,2,0:T(8,128)(2,1)S(1)} %get-tuple-element.156, s32[]{:T(128)} %get-tuple-element.157), kind=kOutput, calls=%fused_computation.3 | convolution fusion | flops 543160320 | bytes 9445380 | tf_op jit(solution)/shard_map/while/body/eval_jaxpr/cond/branch_0_fun/qgpd,kgd->gpqk/dot_general | solution.py:74
  82.6 2.0 %fusion.4 = f32[8,256]{1,0:T(8,128)S(1)} fusion(f32[1024,256,8]{1,0,2:T(8,128)S(1)} %get-tuple-element.264, f32[8,256]{1,0:T(8,128)S(1)} %bitcast.121, pred[256,1024]{0,1:T(8,128)(4,1)S(1)} %broadcast_compare_fusion), kind=kLoop, calls=%fused_computation.5 | loop fusion | flops 10483712 | bytes 8667136 | tf_op jit(solution)/shard_map/while/body/eval_jaxpr/cond/branch_0_fun/reduce_sum | solution.py:82
  84.7 3.7 %fusion.12 = f32[1,8,256,128]{3,2,1,0:T(8,128)S(1)} fusion(f32[1024,256,8]{1,0,2:T(8,128)S(1)} %get-tuple-element.264, f32[8,256]{1,0:T(8,128)S(1)} %bitcast.122, pred[256,1024]{0,1:T(8,128)(4,1)S(1)} %broadcast_compare_fusion, f32[1,8,256,128]{3,2,1,0:T(8,128)S(1)} %get-tuple-element.160, f32[8,256]{1,0:T(8,128)S(1)} %get-tuple-element.259, ...), kind=kOutput, calls=%fused_computation.10 | convolution fusion | flops 547880960 | bytes 11026944 | tf_op jit(solution)/shard_map/while/body/eval_jaxpr/cond/branch_0_fun/gpqk,kgd->gpqd/dot_general | solution.py:83
  88.4 0.6 fusion.137
  90.3 7.4 %conditional.3 = (f32[1,8,256]{2,1,0:T(8,128)S(1)}, f32[1,8,256]{2,1,0:T(8,128)S(1)}, f32[1,8,256,128]{3,2,1,0:T(8,128)S(1)}) conditional(s32[]{:T(128)} %convert_element_type.451, (s32[]{:T(128)}, s32[1,1024]{1,0:T(1,128)S(1)}, bf16[4,1024,1,128]{3,1,2,0:T(8,128)(2,1)S(1)}, s32[]{:T(128)}, bf16[256,1,8,128]{3,0,2,1:T(8,128)(2,1)S(1)}, ...), branch_computations={%region_5.7_spmd, %region_8.8_spmd} | conditional | flops 1101797632 | bytes 29482528 | solution.py:134
  90.4 0.2 broadcast_compare_fusion
  90.6 1.4 %fusion.2 = (f32[8,256]{1,0:T(8,128)S(1)}, f32[1024,256,8]{1,0,2:T(8,128)S(1)}) fusion(pred[256,1024]{0,1:T(8,128)(4,1)S(1)} %broadcast_compare_fusion, bf16[256,1,8,128]{3,0,2,1:T(8,128)(2,1)S(1)} %get-tuple-element.158, bf16[4,1024,1,128]{3,1,2,0:T(8,128)(2,1)S(1)} %get-tuple-element.156, s32[]{:T(128)} %get-tuple-element.157), kind=kOutput, calls=%fused_computation.3 | convolution fusion | flops 543160320 | bytes 9445380 | tf_op jit(solution)/shard_map/while/body/eval_jaxpr/cond/branch_0_fun/qgpd,kgd->gpqk/dot_general | solution.py:74
  92.0 2.0 %fusion.4 = f32[8,256]{1,0:T(8,128)S(1)} fusion(f32[1024,256,8]{1,0,2:T(8,128)S(1)} %get-tuple-element.264, f32[8,256]{1,0:T(8,128)S(1)} %bitcast.121, pred[256,1024]{0,1:T(8,128)(4,1)S(1)} %broadcast_compare_fusion), kind=kLoop, calls=%fused_computation.5 | loop fusion | flops 10483712 | bytes 8667136 | tf_op jit(solution)/shard_map/while/body/eval_jaxpr/cond/branch_0_fun/reduce_sum | solution.py:82
  94.1 3.7 %fusion.12 = f32[1,8,256,128]{3,2,1,0:T(8,128)S(1)} fusion(f32[1024,256,8]{1,0,2:T(8,128)S(1)} %get-tuple-element.264, f32[8,256]{1,0:T(8,128)S(1)} %bitcast.122, pred[256,1024]{0,1:T(8,128)(4,1)S(1)} %broadcast_compare_fusion, f32[1,8,256,128]{3,2,1,0:T(8,128)S(1)} %get-tuple-element.160, f32[8,256]{1,0:T(8,128)S(1)} %get-tuple-element.259, ...), kind=kOutput, calls=%fused_computation.10 | convolution fusion | flops 547880960 | bytes 11026944 | tf_op jit(solution)/shard_map/while/body/eval_jaxpr/cond/branch_0_fun/gpqk,kgd->gpqd/dot_general | solution.py:83
  97.8 0.6 fusion.137
  99.7 7.4 %conditional.3 = (f32[1,8,256]{2,1,0:T(8,128)S(1)}, f32[1,8,256]{2,1,0:T(8,128)S(1)}, f32[1,8,256,128]{3,2,1,0:T(8,128)S(1)}) conditional(s32[]{:T(128)} %convert_element_type.451, (s32[]{:T(128)}, s32[1,1024]{1,0:T(1,128)S(1)}, bf16[4,1024,1,128]{3,1,2,0:T(8,128)(2,1)S(1)}, s32[]{:T(128)}, bf16[256,1,8,128]{3,0,2,1:T(8,128)(2,1)S(1)}, ...), branch_computations={%region_5.7_spmd, %region_8.8_spmd} | conditional | flops 1101797632 | bytes 29482528 | solution.py:134
  99.7 0.2 broadcast_compare_fusion
  100.0 1.4 %fusion.2 = (f32[8,256]{1,0:T(8,128)S(1)}, f32[1024,256,8]{1,0,2:T(8,128)S(1)}) fusion(pred[256,1024]{0,1:T(8,128)(4,1)S(1)} %broadcast_compare_fusion, bf16[256,1,8,128]{3,0,2,1:T(8,128)(2,1)S(1)} %get-tuple-element.158, bf16[4,1024,1,128]{3,1,2,0:T(8,128)(2,1)S(1)} %get-tuple-element.156, s32[]{:T(128)} %get-tuple-element.157), kind=kOutput, calls=%fused_computation.3 | convolution fusion | flops 543160320 | bytes 9445380 | tf_op jit(solution)/shard_map/while/body/eval_jaxpr/cond/branch_0_fun/qgpd,kgd->gpqk/dot_general | solution.py:74
  101.4 2.0 %fusion.4 = f32[8,256]{1,0:T(8,128)S(1)} fusion(f32[1024,256,8]{1,0,2:T(8,128)S(1)} %get-tuple-element.264, f32[8,256]{1,0:T(8,128)S(1)} %bitcast.121, pred[256,1024]{0,1:T(8,128)(4,1)S(1)} %broadcast_compare_fusion), kind=kLoop, calls=%fused_computation.5 | loop fusion | flops 10483712 | bytes 8667136 | tf_op jit(solution)/shard_map/while/body/eval_jaxpr/cond/branch_0_fun/reduce_sum | solution.py:82
  103.5 3.7 %fusion.12 = f32[1,8,256,128]{3,2,1,0:T(8,128)S(1)} fusion(f32[1024,256,8]{1,0,2:T(8,128)S(1)} %get-tuple-element.264, f32[8,256]{1,0:T(8,128)S(1)} %bitcast.122, pred[256,1024]{0,1:T(8,128)(4,1)S(1)} %broadcast_compare_fusion, f32[1,8,256,128]{3,2,1,0:T(8,128)S(1)} %get-tuple-element.160, f32[8,256]{1,0:T(8,128)S(1)} %get-tuple-element.259, ...), kind=kOutput, calls=%fused_computation.10 | convolution fusion | flops 547880960 | bytes 11026944 | tf_op jit(solution)/shard_map/while/body/eval_jaxpr/cond/branch_0_fun/gpqk,kgd->gpqd/dot_general | solution.py:83
  107.2 0.3 copy.60
  107.5 3.1 %fusion.44 = bf16[1,8,256,128]{2,3,1,0:T(8,128)(2,1)S(1)} fusion(f32[8,256,128]{1,2,0:T(8,128)} %fusion.55, f32[8,256,256]{1,2,0:T(8,128)} %get-tuple-element.282, pred[256,256]{0,1:T(8,128)(4,1)S(1)} %iota_compare_fusion, f32[1,8,256,128]{2,3,1,0:T(8,128)S(1)} %copy.60, f32[8,256]{1,0:T(8,128)S(1)} %bitcast.127, f32[8,256]{1,0:T(8,128)S(1)} %fusion.106, ...), kind=kOutput, calls=%fused_computation.39 | convolution fusion | flops 807927808 | bytes 4866048 | tf_op jit(solution)/shard_map/gpts,sgd->gptd/dot_general | solution.py:169
  110.6 1.0 copy.61
  (47 shorter events, 1.6 us)
Async XLA Ops:
  6.5 1.0 copy-start
  6.5 57.3 %all-gather.5.cloned.1.call-start = ((), (), s32[]{:S(2)}) async-start(), calls=%async_computation | async-start | bytes 2228224 | tf_op jit(solution)/shard_map/all_gather | solution.py:23
Sparse Core Ops, SparseCore 0:
  9.5 41.2 all-gather.4
where the time goes:
time: 119 us; the launch traced here: 118 us
  blocking collectives  43.1 us (36%)
  matrix products  30.5 us (26%)
  other arithmetic  13.9 us (12%)
  between operations  13.6 us (11%)
  local copies, waits for them, and re-layouts  11.7 us (10%)
  loops' own time  5.55 us (5%)
    all_gather x4, blocking collectives, prefix_by_axis(): lax.all_gather(part.astype(kind), axis)  43.1 us
    dot_general x4, matrix products, attend(): jnp.einsum('gpqk,kgd->gpqd', weights.astype(jnp.bfloat16), value_block, p...  14.6 us
    reduce_sum x4, other arithmetic, attend(): weight_sum = weight_sum * factor + jnp.sum(weights, axis=-1)  8.15 us
    unnamed x19, local copies, waits for them, and re-layouts  7.44 us
    dot_general x4, matrix products, attend(): jnp.einsum('qgpd,kgd->gpqk', query_block, key_block, preferred_element_ty...  5.64 us
    another operation x1, loops' own time, per_device(): lax.scan(advance, running_state, (key_blocks, value_blocks, key_place))  5.28 us
    dot_general x1, matrix products, per_device(): jnp.einsum('gpts,sgd->gptd', inner_block, values_wide, precision=highest)  3.09 us
    dot_general x2, matrix products, feature_map(): jnp.einsum('thd,hde->hte', inputs, weights, preferred_element_type=jnp.fl...  2.85 us
  transfers between devices with their start and end apart: 1, of which 0 were waited for; matrix products, arithmetic and copies ran while one was open for 9% of the time, Pallas kernels for 0%

commit v1 on v0

v1 whole, which is shorter than its diff:
```python
import math

import jax
import jax.numpy as jnp
from jax import lax
from jax.experimental import pallas as pl
from jax.experimental.pallas import tpu as pltpu
from jax.sharding import Mesh
from jax.sharding import PartitionSpec as P

QHEADS = 128
KVH = 8
LENGTH = 131072
HD = 128
ROWS = 272
TOK = 256
epsilon = 1e-06
masked_score = -1e30
to_exp2 = math.log2(math.e) / math.sqrt(HD)

SWAP = [(0, 1), (1, 0)]


def ring(shift):
    return [(i, (i + shift) % 8) for i in range(8)]


def call(kernel, out_shape, scratch=(), flops=0, nbytes=0, transcendentals=0, name=None):
    return pl.pallas_call(
        kernel,
        out_shape=out_shape,
        scratch_shapes=list(scratch),
        name=name,
        compiler_params=pltpu.CompilerParams(vmem_limit_bytes=40 * 1024 * 1024),
        cost_estimate=pl.CostEstimate(
            flops=flops, bytes_accessed=nbytes, transcendentals=transcendentals
        ),
    )


def first_group(local_heads):
    return lax.axis_index("head") * local_heads // (QHEADS // KVH)


def pack_kernel(keys_ref, values_ref, pos_ref, out_ref, sems):
    g = pl.multiple_of(first_group(8) * HD, HD)
    ck = pltpu.make_async_copy(keys_ref.at[:, pl.ds(g, HD)], out_ref.at[0:TOK, 0:HD], sems.at[0])
    cv = pltpu.make_async_copy(
        values_ref.at[:, pl.ds(g, HD)], out_ref.at[0:TOK, HD : 2 * HD], sems.at[1]
    )
    ck.start()
    cv.start()
    p = pos_ref[...]
    row = lax.broadcasted_iota(jnp.int32, (16, TOK), 0)
    digit = jnp.where(row == 0, p & 255, jnp.where(row == 1, (p >> 8) & 255, p >> 16))
    digit = jnp.where(row < 3, digit, 0)
    out_ref[TOK:ROWS, :] = digit.astype(jnp.float32).astype(jnp.bfloat16)
    ck.wait()
    cv.wait()


def angles_of(block_ref, base=0):
    d = block_ref[base + TOK : base + ROWS, :].astype(jnp.float32)
    p = d[0:1, :] + 256.0 * d[1:2, :] + 65536.0 * d[2:3, :]
    a = (0.5 * math.pi / LENGTH) * p
    return jnp.cos(a), jnp.sin(a)


def elu1(x):
    return jnp.where(x > 0.0, x + 1.0, jnp.exp(jnp.minimum(x, 0.0)))


def dot(a, b, dims):
    return lax.dot_general(a, b, (dims, ((), ())), preferred_element_type=jnp.float32)


def nn(a, b):
    return dot(a, b, ((1,), (0,)))


def nt(a, b):
    return dot(a, b, ((1,), (1,)))


def key_feats_t(block_ref, key_map):
    c, s = angles_of(block_ref)
    phi = elu1(dot(key_map, block_ref[0:TOK, 0:HD], ((0,), (1,))))
    return jnp.concatenate([c * phi, s * phi], axis=0).astype(jnp.bfloat16)


def with_ones(v):
    return jnp.concatenate([v, jnp.ones(v.shape, v.dtype)], axis=1)


def local_kernel(own_ref, q_ref, qmap_ref, kmap_ref, qf_ref, m_ref, accl_ref, stu_ref):
    k = own_ref[0:TOK, 0:HD]
    va = with_ones(own_ref[0:TOK, HD : 2 * HD])
    c, s = angles_of(own_ref)
    ct = jnp.broadcast_to(c, (HD, TOK)).T
    st = jnp.broadcast_to(s, (HD, TOK)).T
    kft = key_feats_t(own_ref, kmap_ref[first_group(8)])
    causal = lax.broadcasted_iota(jnp.int32, (TOK, TOK), 0) >= lax.broadcasted_iota(
        jnp.int32, (TOK, TOK), 1
    )
    for h in range(8):
        q = q_ref[:, h * HD : (h + 1) * HD]
        phi = elu1(nn(q, qmap_ref[h]))
        qf = jnp.concatenate([ct * phi, st * phi], axis=1).astype(jnp.bfloat16)
        qf_ref[h] = qf
        inner = jnp.where(causal, nn(qf, kft), 0.0).astype(jnp.bfloat16)
        stu_ref[h] = nn(inner, va)
        x = jnp.where(causal, nt(q, k), masked_score)
        m = jnp.max(x, axis=1, keepdims=True)
        p = jnp.exp2((x - m) * to_exp2).astype(jnp.bfloat16)
        accl_ref[h] = nn(p, va)
        m_ref[h] = jnp.broadcast_to(m, (TOK, HD))


def absorb(block_refs, q_ref, m_ref, accl_ref):
    for h in range(8):
        q = q_ref[:, h * HD : (h + 1) * HD]
        xs = [nt(q, b[0:TOK, 0:HD]) for b in block_refs]
        m0 = m_ref[h]
        top = jnp.max(xs[0], axis=1, keepdims=True)
        for x in xs[1:]:
            top = jnp.maximum(top, jnp.max(x, axis=1, keepdims=True))
        m1 = jnp.maximum(m0, jnp.broadcast_to(top, m0.shape))
        f = jnp.exp2((m0 - m1) * to_exp2)
        acc = accl_ref[h] * jnp.concatenate([f, f], axis=1)
        mm = jnp.concatenate([m1, m1], axis=1)
        for x, b in zip(xs, block_refs):
            p = jnp.exp2((x - mm) * to_exp2).astype(jnp.bfloat16)
            acc = acc + nn(p, with_ones(b[0:TOK, HD : 2 * HD]))
        accl_ref[h] = acc
        m_ref[h] = m1


def gather_state(block_refs, kmap_ref, state_ref):
    km = kmap_ref[first_group(8)]
    add = None
    for b in block_refs:
        part = nn(key_feats_t(b, km), with_ones(b[0:TOK, HD : 2 * HD]))
        add = part if add is None else add + part
    state_ref[...] += add


def validity():
    z = lax.axis_index("z")
    return {
        "u": lambda k: z >= k,
        "d": lambda k: z >= 8 - k,
        "x": z >= 4,
    }


def mid_kernel(pb, u1, u1s, d1, d1s, x, xs, u2, u2s, d2, d2s, q_ref, kmap_ref, m_in, accl_in,
               m_ref, accl_ref, state_ref):
    m_ref[...] = m_in[...]
    accl_ref[...] = accl_in[...]
    state_ref[...] = jnp.zeros_like(state_ref)
    ok = validity()

    def take(when, *blocks):
        @pl.when(when)
        def _():
            gather_state(blocks, kmap_ref, state_ref)
            absorb(blocks, q_ref, m_ref, accl_ref)

    take(lax.axis_index("c") == 1, pb)
    take(ok["u"](1), u1, u1s)
    take(ok["d"](1), d1, d1s)
    take(ok["x"], x, xs)
    take(ok["u"](2), u2, u2s)
    take(ok["d"](2), d2, d2s)


def last_kernel(u3, u3s, d3, d3s, q_ref, kmap_ref, qf_ref, stu_ref, m_in, accl_in, state_in,
                out_ref, m_ref, accl_ref, state_ref):
    m_ref[...] = m_in[...]
    accl_ref[...] = accl_in[...]
    state_ref[...] = state_in[...]
    ok = validity()

    def take(when, *blocks):
        @pl.when(when)
        def _():
            gather_state(blocks, kmap_ref, state_ref)
            absorb(blocks, q_ref, m_ref, accl_ref)

    take(ok["u"](3), u3, u3s)
    take(ok["d"](3), d3, d3s)
    state = state_ref[...]
    high = state.astype(jnp.bfloat16)
    low = (state - high.astype(jnp.float32)).astype(jnp.bfloat16)
    for h in range(8):
        qf = qf_ref[h]
        nd = stu_ref[h] + nn(qf, high) + nn(qf, low)
        student = nd[:, 0:HD] / (nd[:, HD:] + epsilon)
        accl = accl_ref[h]
        teacher = (accl[:, 0:HD] / accl[:, HD:]).astype(jnp.bfloat16).astype(jnp.float32)
        out_ref[:, h * HD : (h + 1) * HD] = (2.0 * (student - teacher)).astype(jnp.bfloat16)


def per_device(queries, keys, values, query_map, key_map, positions):
    f32, bf16 = jnp.float32, jnp.bfloat16
    any_ = pl.BlockSpec(memory_space=pl.ANY)
    vm = pl.BlockSpec(memory_space=pltpu.VMEM)
    own = pl.pallas_call(
        pack_kernel,
        out_shape=jax.ShapeDtypeStruct((ROWS, 2 * HD), bf16),
        in_specs=[any_, any_, vm],
        out_specs=vm,
        scratch_shapes=[pltpu.SemaphoreType.DMA((2,))],
        name="pack",
    )(keys, values, positions.reshape(1, TOK))
    swap = lambda a: lax.ppermute(a, "c", SWAP)
    u1 = lax.ppermute(own, "z", ring(1))
    d1 = lax.ppermute(own, "z", ring(-1))
    x4 = lax.ppermute(own, "z", ring(4))
    u2 = lax.ppermute(u1, "z", ring(1))
    d2 = lax.ppermute(d1, "z", ring(-1))
    u3 = lax.ppermute(u2, "z", ring(1))
    d3 = lax.ppermute(d2, "z", ring(-1))

    heads = lambda w, t: jax.ShapeDtypeStruct((8, TOK, w), t)
    state = jax.ShapeDtypeStruct((2 * HD, 2 * HD), f32)
    qf, m, accl, stu = call(
        local_kernel,
        (heads(256, bf16), heads(HD, f32), heads(256, f32), heads(256, f32)),
        flops=8 * 2 * 256 * 128 * 1500,
        nbytes=8 << 20,
        name="own",
    )(own, queries, query_map, key_map)
    arrivals = [swap(own)]
    for a in (u1, d1, x4, u2, d2):
        arrivals += [a, swap(a)]
    m, accl, st = call(
        mid_kernel,
        (heads(HD, f32), heads(256, f32), state),
        flops=8 * 2 * 256 * 128 * 6000,
        nbytes=8 << 20,
        name="mid",
    )(*arrivals, queries, key_map, m, accl)
    tail = [u3, swap(u3), d3, swap(d3)]
    return call(
        last_kernel,
        jax.ShapeDtypeStruct((TOK, 8 * HD), bf16),
        scratch=(
            pltpu.VMEM((8, TOK, HD), f32),
            pltpu.VMEM((8, TOK, 256), f32),
            pltpu.VMEM((2 * HD, 2 * HD), f32),
        ),
        flops=8 * 2 * 256 * 128 * 3000,
        nbytes=8 << 20,
        name="last",
    )(*tail, queries, key_map, qf, stu, m, accl, st)


def solution(mesh):
    split = Mesh(mesh.devices.reshape(8, 2, mesh.shape["head"]), ("z", "c", "head"))
    seq = ("z", "c")
    placed = (P(seq, "head"), P(seq, None), P(seq, None), P("head", None, None), P(), P(seq))
    return jax.shard_map(
        per_device, mesh=split, in_specs=placed, out_specs=P(seq, "head"), check_vma=False
    )
```

time: 119 us -> 45.7 us (0.38)
  the two profiles are of different devices: /device:TPU:208 before, /device:TPU:235 now
where the time goes in v1:
time: 45.7 us; the launch traced here: 45.5 us
  Pallas kernels  22.4 us (49%)
  starting transfers between devices  16.7 us (37%)
  local copies, waits for them, and re-layouts  3.85 us (8%)
  waiting for transfers between devices  2.41 us (5%)
    pallas_call x1, Pallas kernels, per_device(): call(mid_kernel, (heads(HD, f32), heads(256, f32), state), flops=8 * 2 *...  11.1 us
    ppermute x8, starting transfers between devices, per_device(): swap = lambda a: lax.ppermute(a, 'c', SWAP)  6.77 us
    pallas_call x1, Pallas kernels, per_device(): call(last_kernel, jax.ShapeDtypeStruct((TOK, 8 * HD), bf16), scratch=(plt...  5.85 us
    unnamed x12, local copies, waits for them, and re-layouts  3.85 us
    pallas_call x1, Pallas kernels, per_device(): call(local_kernel, (heads(256, bf16), heads(HD, f32), heads(256, f32), he...  3.17 us
    ppermute x1, starting transfers between devices, per_device(): u2 = lax.ppermute(u1, 'z', ring(1))  2.95 us
    ppermute x1, starting transfers between devices, per_device(): u3 = lax.ppermute(u2, 'z', ring(1))  2.94 us
    ppermute x1, starting transfers between devices, per_device(): x4 = lax.ppermute(own, 'z', ring(4))  2.55 us
  transfers between devices with their start and end apart: 15, of which 1 were waited for; matrix products, arithmetic and copies ran while one was open for 0% of the time, Pallas kernels for 31%

profile of v1, /device:TPU:235, one launch (start us, length us, event | category | flops | bytes accessed | tf_op | source)
XLA Modules:
  0.0 45.5 jit_solution(14814100512169969127)
XLA Ops:
  0.0 0.0 copy-start.3
  0.0 0.0 copy-start.1
  0.0 2.3 %pack.1.own_ref = bf16[272,256]{1,0:T(8,128)(2,1)} custom-call(bf16[256,1024]{1,0:T(8,128)(2,1)} %keys_ref.1, bf16[256,1024]{1,0:T(8,128)(2,1)} %values_ref.1, s32[1,256]{1,0:T(1,128)} %bitcast.1), custom_call_target="tpu_custom_call" | custom-call | tf_op jit(solution)/shard_map/pack/pallas_call | solution.py:208
  2.3 0.1 collective-permute-start
  2.4 1.5 %collective-permute-start.4 = (bf16[272,256]{1,0:T(8,128)(2,1)}, bf16[272,256]{1,0:T(8,128)(2,1)S(1)}, u32[]{:S(2)}, u32[]{:S(2)}) collective-permute-start(bf16[272,256]{1,0:T(8,128)(2,1)} %pack.1.own_ref), channel_id=1, source_target_pairs={{0,224},{32,0},{64,32},{96,64},{128,96},{160,128},{192,160},{224,1... | collective-permute-start | bytes 417800 | tf_op jit(solution)/shard_map/ppermute | solution.py:218
  3.9 2.5 %collective-permute-start.11 = (bf16[272,256]{1,0:T(8,128)(2,1)}, bf16[272,256]{1,0:T(8,128)(2,1)S(1)}, u32[]{:S(2)}, u32[]{:S(2)}) collective-permute-start(bf16[272,256]{1,0:T(8,128)(2,1)} %pack.1.own_ref), channel_id=1, source_target_pairs={{0,128},{32,160},{64,192},{96,224},{128,0},{160,32},{192,64},{224,... | collective-permute-start | bytes 417800 | tf_op jit(solution)/shard_map/ppermute | solution.py:219
  6.4 1.2 %collective-permute-start.8 = (bf16[272,256]{1,0:T(8,128)(2,1)}, bf16[272,256]{1,0:T(8,128)(2,1)S(1)}, u32[]{:S(2)}, u32[]{:S(2)}) collective-permute-start(bf16[272,256]{1,0:T(8,128)(2,1)} %pack.1.own_ref), channel_id=1, source_target_pairs={{0,16},{16,0},{1,17},{17,1},{2,18},{18,2},{3,19},{19,3},{4,20},{20... | collective-permute-start | bytes 417800 | tf_op jit(solution)/shard_map/ppermute | solution.py:216
  7.6 0.0 collective-permute-done.u1
  7.6 3.0 %collective-permute-start.1 = (bf16[272,256]{1,0:T(8,128)(2,1)S(1)}, bf16[272,256]{1,0:T(8,128)(2,1)S(1)}, u32[]{:S(2)}, u32[]{:S(2)}) collective-permute-start(bf16[272,256]{1,0:T(8,128)(2,1)S(1)} %collective-permute-done.u1), channel_id=1, source_target_pairs={{0,32},{32,64},{64,96},{96,128},{128,160},{160,192},{192,224},{224... | collective-permute-start | bytes 417800 | tf_op jit(solution)/shard_map/ppermute | solution.py:220
  10.6 0.0 collective-permute-done.4.d1
  10.6 0.0 collective-permute-start.5
  10.6 1.2 %collective-permute-start.10 = (bf16[272,256]{1,0:T(8,128)(2,1)S(1)}, bf16[272,256]{1,0:T(8,128)(2,1)S(1)}, u32[]{:S(2)}, u32[]{:S(2)}) collective-permute-start(bf16[272,256]{1,0:T(8,128)(2,1)S(1)} %collective-permute-done.4.d1), channel_id=1, source_target_pairs={{0,16},{16,0},{1,17},{17,1},{2,18},{18,2},{3,19},{19,3},{4,20},{20... | collective-permute-start | bytes 417800 | tf_op jit(solution)/shard_map/ppermute | solution.py:216
  11.9 2.4 %collective-permute-done.11.x = bf16[272,256]{1,0:T(8,128)(2,1)S(1)} collective-permute-done((bf16[272,256]{1,0:T(8,128)(2,1)}, bf16[272,256]{1,0:T(8,128)(2,1)S(1)}, u32[]{:S(2)}, u32[]{:S(2)}) %collective-permute-start.11) | collective-permute-done | bytes 139296 | tf_op jit(solution)/shard_map/ppermute | solution.py:219
  14.2 2.4 %collective-permute-start.9 = (bf16[272,256]{1,0:T(8,128)(2,1)S(1)}, bf16[272,256]{1,0:T(8,128)(2,1)S(1)}, u32[]{:S(2)}, u32[]{:S(2)}) collective-permute-start(bf16[272,256]{1,0:T(8,128)(2,1)S(1)} %collective-permute-done.u1), channel_id=1, source_target_pairs={{0,16},{16,0},{1,17},{17,1},{2,18},{18,2},{3,19},{19,3},{4,20},{20... | collective-permute-start | bytes 417800 | tf_op jit(solution)/shard_map/ppermute | solution.py:216
  16.6 0.0 collective-permute-done.8.pb
  16.6 0.0 collective-permute-start.12
  16.6 0.0 collective-permute-done.1.u2
  16.7 2.9 %collective-permute-start.2 = (bf16[272,256]{1,0:T(8,128)(2,1)S(1)}, bf16[272,256]{1,0:T(8,128)(2,1)S(1)}, u32[]{:S(2)}, u32[]{:S(2)}) collective-permute-start(bf16[272,256]{1,0:T(8,128)(2,1)S(1)} %collective-permute-done.1.u2), channel_id=1, source_target_pairs={{0,32},{32,64},{64,96},{96,128},{128,160},{160,192},{192,224},{224... | collective-permute-start | bytes 417800 | tf_op jit(solution)/shard_map/ppermute | solution.py:222
  19.6 0.0 collective-permute-done.5.d2
  19.6 0.0 collective-permute-start.6
  19.6 0.0 collective-permute-done.10.d1s
  19.6 1.0 %collective-permute-start.13 = (bf16[272,256]{1,0:T(8,128)(2,1)S(1)}, bf16[272,256]{1,0:T(8,128)(2,1)S(1)}, u32[]{:S(2)}, u32[]{:S(2)}) collective-permute-start(bf16[272,256]{1,0:T(8,128)(2,1)S(1)} %collective-permute-done.1.u2), channel_id=1, source_target_pairs={{0,16},{16,0},{1,17},{17,1},{2,18},{18,2},{3,19},{19,3},{4,20},{20... | collective-permute-start | bytes 417800 | tf_op jit(solution)/shard_map/ppermute | solution.py:216
  20.6 0.0 collective-permute-done.9.u1s
  20.6 0.1 collective-permute-start.14
  20.7 0.0 copy-start
  20.7 1.0 %copy-done = bf16[256,1024]{1,0:T(8,128)(2,1)S(1)} copy-done((bf16[256,1024]{1,0:T(8,128)(2,1)S(1)}, bf16[256,1024]{1,0:T(8,128)(2,1)}, u32[]{:S(2)}) %copy-start) | copy-done | bytes 524312
  21.7 0.0 copy-start.2
  21.7 0.9 %copy-done.2 = bf16[8,128,128]{2,1,0:T(8,128)(2,1)S(1)} copy-done((bf16[8,128,128]{2,1,0:T(8,128)(2,1)S(1)}, bf16[8,128,128]{2,1,0:T(8,128)(2,1)}, u32[]{:S(2)}) %copy-start.2) | copy-done | bytes 262168
  22.7 0.0 copy-start.4
  22.7 0.9 %copy-done.4 = bf16[272,256]{1,0:T(8,128)(2,1)S(1)} copy-done((bf16[272,256]{1,0:T(8,128)(2,1)S(1)}, bf16[272,256]{1,0:T(8,128)(2,1)}, u32[]{:S(2)}) %copy-start.4) | copy-done | bytes 139288
  23.6 0.0 copy-start.5
  23.6 0.9 %copy-done.5 = bf16[8,128,128]{2,1,0:T(8,128)(2,1)S(1)} copy-done((bf16[8,128,128]{2,1,0:T(8,128)(2,1)S(1)}, bf16[8,128,128]{2,1,0:T(8,128)(2,1)}, u32[]{:S(2)}) %copy-start.5) | copy-done | bytes 262168
  24.6 3.2 %own.1 = (bf16[8,256,256]{2,1,0:T(8,128)(2,1)S(1)}, f32[8,256,128]{2,1,0:T(8,128)S(1)}, f32[8,256,256]{2,1,0:T(8,128)S(1)}, f32[8,256,256]{2,1,0:T(8,128)S(1)}) custom-call(bf16[272,256]{1,0:T(8,128)(2,1)S(1)} %copy-done.4, bf16[256,1024]{1,0:T(8,128)(2,1)S(1)} %copy-done, bf16[8,128,128]{2,1,0:T(8,128)(2,1)S(1)} %copy-done.5, bf16[8,128,128]{2,1,0:T(8,128)(2,1)S(1)} %copy-done.2), custom_call_target="tpu_custom_call" | custom-call | flops 786432000 | bytes 8388608 | tf_op jit(solution)/shard_map/own/pallas_call | solution.py:227
  27.7 0.0 collective-permute-done.2.u3
  27.7 0.5 %collective-permute-start.3 = (bf16[272,256]{1,0:T(8,128)(2,1)S(1)}, bf16[272,256]{1,0:T(8,128)(2,1)S(1)}, u32[]{:S(2)}, u32[]{:S(2)}) collective-permute-start(bf16[272,256]{1,0:T(8,128)(2,1)S(1)} %collective-permute-done.2.u3), channel_id=1, source_target_pairs={{0,16},{16,0},{1,17},{17,1},{2,18},{18,2},{3,19},{19,3},{4,20},{20... | collective-permute-start | bytes 417800 | tf_op jit(solution)/shard_map/ppermute | solution.py:216
  28.2 0.0 collective-permute-done.6.d3
  28.2 0.3 collective-permute-start.7
  28.5 0.0 collective-permute-done.12.xs
  28.5 0.0 collective-permute-done.13.u2s
  28.5 0.0 collective-permute-done.14.d2s
  28.5 0.0 copy-done.3
  28.5 0.0 copy-done.1
  28.5 11.1 %mid.1 = (f32[8,256,128]{2,1,0:T(8,128)S(1)}, f32[8,256,256]{2,1,0:T(8,128)S(1)}, f32[256,256]{1,0:T(8,128)S(1)}) custom-call(bf16[272,256]{1,0:T(8,128)(2,1)S(1)} %collective-permute-done.8.pb, bf16[272,256]{1,0:T(8,128)(2,1)S(1)} %collective-permute-done.u1, bf16[272,256]{1,0:T(8,128)(2,1)S(1)} %collective-permute-done.9.u1s, ...), custom_call_target="tpu_custom_call" | custom-call | flops 3145728000 | bytes 8388608 | tf_op jit(solution)/shard_map/mid/pallas_call | solution.py:237
  39.6 0.0 collective-permute-done.3.u3s
  39.6 0.0 collective-permute-done.7.d3s
  39.6 5.9 %last.1 = bf16[256,1024]{1,0:T(8,128)(2,1)} custom-call(bf16[272,256]{1,0:T(8,128)(2,1)S(1)} %collective-permute-done.2.u3, bf16[272,256]{1,0:T(8,128)(2,1)S(1)} %collective-permute-done.3.u3s, bf16[272,256]{1,0:T(8,128)(2,1)S(1)} %collective-permute-done.6.d3, bf16[272,256]{1,0:T(8,128)(2,1)S(1)} %collective-permute-done.7.d3s, ...), custom_call_target="tpu_custom_call" | custom-call | flops 1572864000 | bytes 8388608 | tf_op jit(solution)/shard_map/last/pallas_call | solution.py:245
Async XLA Ops:
  0.0 28.5 %copy-start.3 = (bf16[8,128,128]{2,1,0:T(8,128)(2,1)S(1)}, bf16[8,128,128]{2,1,0:T(8,128)(2,1)}, u32[]{:S(2)}) copy-start(bf16[8,128,128]{2,1,0:T(8,128)(2,1)} %kmap_ref.5) | copy-start | bytes 786436
  0.0 28.5 %copy-start.1 = (bf16[256,1024]{1,0:T(8,128)(2,1)S(1)}, bf16[256,1024]{1,0:T(8,128)(2,1)}, u32[]{:S(2)}) copy-start(bf16[256,1024]{1,0:T(8,128)(2,1)} %q_ref.5) | copy-start | bytes 1572868
  2.3 5.3 %collective-permute-start = (bf16[272,256]{1,0:T(8,128)(2,1)}, bf16[272,256]{1,0:T(8,128)(2,1)S(1)}, u32[]{:S(2)}, u32[]{:S(2)}) collective-permute-start(bf16[272,256]{1,0:T(8,128)(2,1)} %pack.1.own_ref), channel_id=1, source_target_pairs={{0,32},{32,64},{64,96},{96,128},{128,160},{160,192},{192,224},{224... | collective-permute-start | bytes 417800 | tf_op jit(solution)/shard_map/ppermute | solution.py:217
  2.4 8.2 %collective-permute-start.4 = (bf16[272,256]{1,0:T(8,128)(2,1)}, bf16[272,256]{1,0:T(8,128)(2,1)S(1)}, u32[]{:S(2)}, u32[]{:S(2)}) collective-permute-start(bf16[272,256]{1,0:T(8,128)(2,1)} %pack.1.own_ref), channel_id=1, source_target_pairs={{0,224},{32,0},{64,32},{96,64},{128,96},{160,128},{192,160},{224,1... | collective-permute-start | bytes 417800 | tf_op jit(solution)/shard_map/ppermute | solution.py:218
  3.9 10.4 %collective-permute-start.11 = (bf16[272,256]{1,0:T(8,128)(2,1)}, bf16[272,256]{1,0:T(8,128)(2,1)S(1)}, u32[]{:S(2)}, u32[]{:S(2)}) collective-permute-start(bf16[272,256]{1,0:T(8,128)(2,1)} %pack.1.own_ref), channel_id=1, source_target_pairs={{0,128},{32,160},{64,192},{96,224},{128,0},{160,32},{192,64},{224,... | collective-permute-start | bytes 417800 | tf_op jit(solution)/shard_map/ppermute | solution.py:219
  6.4 10.2 %collective-permute-start.8 = (bf16[272,256]{1,0:T(8,128)(2,1)}, bf16[272,256]{1,0:T(8,128)(2,1)S(1)}, u32[]{:S(2)}, u32[]{:S(2)}) collective-permute-start(bf16[272,256]{1,0:T(8,128)(2,1)} %pack.1.own_ref), channel_id=1, source_target_pairs={{0,16},{16,0},{1,17},{17,1},{2,18},{18,2},{3,19},{19,3},{4,20},{20... | collective-permute-start | bytes 417800 | tf_op jit(solution)/shard_map/ppermute | solution.py:216
  7.6 9.0 %collective-permute-start.1 = (bf16[272,256]{1,0:T(8,128)(2,1)S(1)}, bf16[272,256]{1,0:T(8,128)(2,1)S(1)}, u32[]{:S(2)}, u32[]{:S(2)}) collective-permute-start(bf16[272,256]{1,0:T(8,128)(2,1)S(1)} %collective-permute-done.u1), channel_id=1, source_target_pairs={{0,32},{32,64},{64,96},{96,128},{128,160},{160,192},{192,224},{224... | collective-permute-start | bytes 417800 | tf_op jit(solution)/shard_map/ppermute | solution.py:220
  10.6 9.0 %collective-permute-start.5 = (bf16[272,256]{1,0:T(8,128)(2,1)S(1)}, bf16[272,256]{1,0:T(8,128)(2,1)S(1)}, u32[]{:S(2)}, u32[]{:S(2)}) collective-permute-start(bf16[272,256]{1,0:T(8,128)(2,1)S(1)} %collective-permute-done.4.d1), channel_id=1, source_target_pairs={{0,224},{32,0},{64,32},{96,64},{128,96},{160,128},{192,160},{224,1... | collective-permute-start | bytes 417800 | tf_op jit(solution)/shard_map/ppermute | solution.py:221
  10.6 9.0 %collective-permute-start.10 = (bf16[272,256]{1,0:T(8,128)(2,1)S(1)}, bf16[272,256]{1,0:T(8,128)(2,1)S(1)}, u32[]{:S(2)}, u32[]{:S(2)}) collective-permute-start(bf16[272,256]{1,0:T(8,128)(2,1)S(1)} %collective-permute-done.4.d1), channel_id=1, source_target_pairs={{0,16},{16,0},{1,17},{17,1},{2,18},{18,2},{3,19},{19,3},{4,20},{20... | collective-permute-start | bytes 417800 | tf_op jit(solution)/shard_map/ppermute | solution.py:216
  14.2 6.4 %collective-permute-start.9 = (bf16[272,256]{1,0:T(8,128)(2,1)S(1)}, bf16[272,256]{1,0:T(8,128)(2,1)S(1)}, u32[]{:S(2)}, u32[]{:S(2)}) collective-permute-start(bf16[272,256]{1,0:T(8,128)(2,1)S(1)} %collective-permute-done.u1), channel_id=1, source_target_pairs={{0,16},{16,0},{1,17},{17,1},{2,18},{18,2},{3,19},{19,3},{4,20},{20... | collective-permute-start | bytes 417800 | tf_op jit(solution)/shard_map/ppermute | solution.py:216
  16.6 11.9 %collective-permute-start.12 = (bf16[272,256]{1,0:T(8,128)(2,1)S(1)}, bf16[272,256]{1,0:T(8,128)(2,1)S(1)}, u32[]{:S(2)}, u32[]{:S(2)}) collective-permute-start(bf16[272,256]{1,0:T(8,128)(2,1)S(1)} %collective-permute-done.11.x), channel_id=1, source_target_pairs={{0,16},{16,0},{1,17},{17,1},{2,18},{18,2},{3,19},{19,3},{4,20},{20... | collective-permute-start | bytes 417800 | tf_op jit(solution)/shard_map/ppermute | solution.py:216
  16.7 11.1 %collective-permute-start.2 = (bf16[272,256]{1,0:T(8,128)(2,1)S(1)}, bf16[272,256]{1,0:T(8,128)(2,1)S(1)}, u32[]{:S(2)}, u32[]{:S(2)}) collective-permute-start(bf16[272,256]{1,0:T(8,128)(2,1)S(1)} %collective-permute-done.1.u2), channel_id=1, source_target_pairs={{0,32},{32,64},{64,96},{96,128},{128,160},{160,192},{192,224},{224... | collective-permute-start | bytes 417800 | tf_op jit(solution)/shard_map/ppermute | solution.py:222
  19.6 8.6 %collective-permute-start.6 = (bf16[272,256]{1,0:T(8,128)(2,1)S(1)}, bf16[272,256]{1,0:T(8,128)(2,1)S(1)}, u32[]{:S(2)}, u32[]{:S(2)}) collective-permute-start(bf16[272,256]{1,0:T(8,128)(2,1)S(1)} %collective-permute-done.5.d2), channel_id=1, source_target_pairs={{0,224},{32,0},{64,32},{96,64},{128,96},{160,128},{192,160},{224,1... | collective-permute-start | bytes 417800 | tf_op jit(solution)/shard_map/ppermute | solution.py:223
  19.6 8.9 %collective-permute-start.13 = (bf16[272,256]{1,0:T(8,128)(2,1)S(1)}, bf16[272,256]{1,0:T(8,128)(2,1)S(1)}, u32[]{:S(2)}, u32[]{:S(2)}) collective-permute-start(bf16[272,256]{1,0:T(8,128)(2,1)S(1)} %collective-permute-done.1.u2), channel_id=1, source_target_pairs={{0,16},{16,0},{1,17},{17,1},{2,18},{18,2},{3,19},{19,3},{4,20},{20... | collective-permute-start | bytes 417800 | tf_op jit(solution)/shard_map/ppermute | solution.py:216
  20.6 7.9 %collective-permute-start.14 = (bf16[272,256]{1,0:T(8,128)(2,1)S(1)}, bf16[272,256]{1,0:T(8,128)(2,1)S(1)}, u32[]{:S(2)}, u32[]{:S(2)}) collective-permute-start(bf16[272,256]{1,0:T(8,128)(2,1)S(1)} %collective-permute-done.5.d2), channel_id=1, source_target_pairs={{0,16},{16,0},{1,17},{17,1},{2,18},{18,2},{3,19},{19,3},{4,20},{20... | collective-permute-start | bytes 417800 | tf_op jit(solution)/shard_map/ppermute | solution.py:216
  20.7 1.0 %copy-start = (bf16[256,1024]{1,0:T(8,128)(2,1)S(1)}, bf16[256,1024]{1,0:T(8,128)(2,1)}, u32[]{:S(2)}) copy-start(bf16[256,1024]{1,0:T(8,128)(2,1)} %q_ref.5) | copy-start | bytes 1572868
  21.7 0.9 %copy-start.2 = (bf16[8,128,128]{2,1,0:T(8,128)(2,1)S(1)}, bf16[8,128,128]{2,1,0:T(8,128)(2,1)}, u32[]{:S(2)}) copy-start(bf16[8,128,128]{2,1,0:T(8,128)(2,1)} %kmap_ref.5) | copy-start | bytes 786436
  22.7 0.9 %copy-start.4 = (bf16[272,256]{1,0:T(8,128)(2,1)S(1)}, bf16[272,256]{1,0:T(8,128)(2,1)}, u32[]{:S(2)}) copy-start(bf16[272,256]{1,0:T(8,128)(2,1)} %pack.1.own_ref) | copy-start | bytes 417796
  23.6 0.9 %copy-start.5 = (bf16[8,128,128]{2,1,0:T(8,128)(2,1)S(1)}, bf16[8,128,128]{2,1,0:T(8,128)(2,1)}, u32[]{:S(2)}) copy-start(bf16[8,128,128]{2,1,0:T(8,128)(2,1)} %qmap_ref.1) | copy-start | bytes 786436
  27.7 11.9 %collective-permute-start.3 = (bf16[272,256]{1,0:T(8,128)(2,1)S(1)}, bf16[272,256]{1,0:T(8,128)(2,1)S(1)}, u32[]{:S(2)}, u32[]{:S(2)}) collective-permute-start(bf16[272,256]{1,0:T(8,128)(2,1)S(1)} %collective-permute-done.2.u3), channel_id=1, source_target_pairs={{0,16},{16,0},{1,17},{17,1},{2,18},{18,2},{3,19},{19,3},{4,20},{20... | collective-permute-start | bytes 417800 | tf_op jit(solution)/shard_map/ppermute | solution.py:216
  28.2 11.4 %collective-permute-start.7 = (bf16[272,256]{1,0:T(8,128)(2,1)S(1)}, bf16[272,256]{1,0:T(8,128)(2,1)S(1)}, u32[]{:S(2)}, u32[]{:S(2)}) collective-permute-start(bf16[272,256]{1,0:T(8,128)(2,1)S(1)} %collective-permute-done.6.d3), channel_id=1, source_target_pairs={{0,16},{16,0},{1,17},{17,1},{2,18},{18,2},{3,19},{19,3},{4,20},{20... | collective-permute-start | bytes 417800 | tf_op jit(solution)/shard_map/ppermute | solution.py:216

commit v2 on v1

v2 whole, which is shorter than its diff:
```python
import math

import jax
import jax.numpy as jnp
from jax import lax
from jax.experimental import pallas as pl
from jax.experimental.pallas import tpu as pltpu
from jax.sharding import Mesh
from jax.sharding import PartitionSpec as P


QHEADS = 128
KVH = 8
LENGTH = 131072
HD = 128
ROWS = 272
TOK = 256
epsilon = 1e-06
masked_score = -1e30
to_exp2 = math.log2(math.e) / math.sqrt(HD)

SWAP = [(0, 1), (1, 0)]


def ring(shift):
    return [(i, (i + shift) % 8) for i in range(8)]


def call(kernel, out_shape, in_specs=None, scratch=(), flops=0, nbytes=0, transcendentals=0):
    more = {} if in_specs is None else {"in_specs": in_specs}
    return pl.pallas_call(
        kernel,
        out_shape=out_shape,
        **more,
        scratch_shapes=list(scratch),
        compiler_params=pltpu.CompilerParams(vmem_limit_bytes=40 * 1024 * 1024),
        cost_estimate=pl.CostEstimate(
            flops=flops, bytes_accessed=nbytes, transcendentals=transcendentals
        ),
    )


def first_group(local_heads):
    return lax.axis_index("head") * local_heads // (QHEADS // KVH)


def pieces(x):
    a = x.astype(jnp.bfloat16)
    x = x - a.astype(jnp.float32)
    b = x.astype(jnp.bfloat16)
    c = (x - b.astype(jnp.float32)).astype(jnp.bfloat16)
    return a.astype(jnp.float32), b.astype(jnp.float32), c.astype(jnp.float32)


def pack_kernel(keys_ref, values_ref, pos_ref, out_ref, pos_vmem, sems):
    g = pl.multiple_of(first_group(8) * HD, HD)
    cp = pltpu.make_async_copy(pos_ref, pos_vmem, sems.at[2])
    ck = pltpu.make_async_copy(keys_ref.at[:, pl.ds(g, HD)], out_ref.at[0:TOK, 0:HD], sems.at[0])
    cv = pltpu.make_async_copy(
        values_ref.at[:, pl.ds(g, HD)], out_ref.at[0:TOK, HD : 2 * HD], sems.at[1]
    )
    cp.start()
    ck.start()
    cv.start()
    cp.wait()
    a = (0.5 * math.pi / LENGTH) * pos_vmem[...].astype(jnp.float32)
    row = lax.broadcasted_iota(jnp.int32, (16, TOK), 0)
    tile = jnp.zeros((16, TOK), jnp.float32)
    for i, part in enumerate(pieces(jnp.cos(a)) + pieces(jnp.sin(a))):
        tile = jnp.where(row == i, part, tile)
    out_ref[TOK:ROWS, :] = tile.astype(jnp.bfloat16)
    ck.wait()
    cv.wait()


def angles_of(block_ref):
    d = block_ref[TOK:ROWS, :].astype(jnp.float32)
    return d[0:1] + d[1:2] + d[2:3], d[3:4] + d[4:5] + d[5:6]


def elu1(x):
    return jnp.where(x > 0.0, x + 1.0, jnp.exp(jnp.minimum(x, 0.0)))


def dot(a, b, dims):
    return lax.dot_general(a, b, (dims, ((), ())), preferred_element_type=jnp.float32)


def nn(a, b):
    return dot(a, b, ((1,), (0,)))


def nt(a, b):
    return dot(a, b, ((1,), (1,)))


def key_feats_t(block_ref, key_map, ok=None):
    c, s = angles_of(block_ref)
    if ok is not None:
        c, s = jnp.where(ok, c, 0.0), jnp.where(ok, s, 0.0)
    phi = elu1(dot(key_map, block_ref[0:TOK, 0:HD], ((0,), (1,))))
    return jnp.concatenate([c * phi, s * phi], axis=0).astype(jnp.bfloat16)


def with_ones(v):
    return jnp.concatenate([v, jnp.ones(v.shape, v.dtype)], axis=1)


def local_kernel(own_ref, q_ref, qmap_ref, kmap_ref, qf_ref, m_ref, accl_ref, stu_ref):
    k = own_ref[0:TOK, 0:HD]
    va = with_ones(own_ref[0:TOK, HD : 2 * HD])
    c, s = angles_of(own_ref)
    ct = jnp.broadcast_to(c, (HD, TOK)).T
    st = jnp.broadcast_to(s, (HD, TOK)).T
    kft = key_feats_t(own_ref, kmap_ref[first_group(8)])
    causal = lax.broadcasted_iota(jnp.int32, (TOK, TOK), 0) >= lax.broadcasted_iota(
        jnp.int32, (TOK, TOK), 1
    )
    for h in range(8):
        q = q_ref[:, h * HD : (h + 1) * HD]
        phi = elu1(nn(q, qmap_ref[h]))
        qf = jnp.concatenate([ct * phi, st * phi], axis=1).astype(jnp.bfloat16)
        qf_ref[h] = qf
        inner = jnp.where(causal, nn(qf, kft), 0.0).astype(jnp.bfloat16)
        stu_ref[h] = nn(inner, va)
        x = jnp.where(causal, nt(q, k), masked_score)
        m = jnp.max(x, axis=1, keepdims=True)
        p = jnp.exp2((x - m) * to_exp2).astype(jnp.bfloat16)
        accl_ref[h] = nn(p, va)
        m_ref[h] = jnp.broadcast_to(m, (TOK, HD))


def absorb(blocks, q_ref, kmap_ref, m_ref, accl_ref, state_ref):
    km = kmap_ref[first_group(8)]
    va = jnp.concatenate([with_ones(b[0:TOK, HD : 2 * HD]) for b, _ in blocks], axis=0)
    feats = [None] * len(blocks)
    for h in range(8):
        q = q_ref[:, h * HD : (h + 1) * HD]
        xs = [nt(q, b[0:TOK, 0:HD]) for b, _ in blocks]
        for i in range(h, len(blocks), 8):
            feats[i] = key_feats_t(blocks[i][0], km, blocks[i][1])
        m0 = m_ref[h]
        top = None
        for x, (_, ok) in zip(xs, blocks):
            t = jnp.where(ok, jnp.maximum(x[:, 0:HD], x[:, HD:]), masked_score)
            top = t if top is None else jnp.maximum(top, t)
        top = jnp.max(top, axis=1, keepdims=True)
        m1 = jnp.maximum(m0, jnp.broadcast_to(top, m0.shape))
        f = jnp.exp2((m0 - m1) * to_exp2)
        ps = []
        for x, (_, ok) in zip(xs, blocks):
            mm = jnp.where(ok, m1, -masked_score)
            p = jnp.exp2((x - jnp.concatenate([mm, mm], axis=1)) * to_exp2)
            ps.append(p.astype(jnp.bfloat16))
        add = nn(jnp.concatenate(ps, axis=1), va)
        accl_ref[h] = accl_ref[h] * jnp.concatenate([f, f], axis=1) + add
        m_ref[h] = m1
    state_ref[...] += nn(jnp.concatenate(feats, axis=1), va)


def mid_kernel(pb, u1, u1s, d1, d1s, x, xs, u2, u2s, d2, d2s, q_ref, kmap_ref, m_in, accl_in,
               m_ref, accl_ref, state_ref):
    m_ref[...] = m_in[...]
    accl_ref[...] = accl_in[...]
    state_ref[...] = jnp.zeros_like(state_ref)
    z = lax.axis_index("z")
    rest = (q_ref, kmap_ref, m_ref, accl_ref, state_ref)
    second = lax.axis_index("c") == 1
    absorb(
        [(pb, second), (u1, z >= 1), (u1s, z >= 1), (x, z >= 4), (xs, z >= 4), (u2, z >= 2),
         (u2s, z >= 2)],
        *rest,
    )

    @pl.when(z >= 6)
    def _():
        absorb([(d1, z >= 7), (d1s, z >= 7), (d2, z >= 6), (d2s, z >= 6)], *rest)


def last_kernel(u3, u3s, d3, d3s, q_ref, kmap_ref, qf_ref, stu_ref, m_in, accl_in, state_in,
                out_ref, m_ref, accl_ref, state_ref):
    m_ref[...] = m_in[...]
    accl_ref[...] = accl_in[...]
    state_ref[...] = state_in[...]
    z = lax.axis_index("z")
    rest = (q_ref, kmap_ref, m_ref, accl_ref, state_ref)

    @pl.when(z >= 5)
    def _():
        absorb([(u3, z >= 3), (u3s, z >= 3), (d3, z >= 5), (d3s, z >= 5)], *rest)

    @pl.when((z >= 3) & (z < 5))
    def _():
        absorb([(u3, z >= 3), (u3s, z >= 3)], *rest)

    state = state_ref[...]
    high = state.astype(jnp.bfloat16)
    low = (state - high.astype(jnp.float32)).astype(jnp.bfloat16)
    for h in range(8):
        qf = qf_ref[h]
        nd = stu_ref[h] + nn(qf, high) + nn(qf, low)
        student = nd[:, 0:HD] / (nd[:, HD:] + epsilon)
        accl = accl_ref[h]
        teacher = (accl[:, 0:HD] / accl[:, HD:]).astype(jnp.bfloat16).astype(jnp.float32)
        out_ref[:, h * HD : (h + 1) * HD] = (2.0 * (student - teacher)).astype(jnp.bfloat16)


def per_device(queries, keys, values, query_map, key_map, positions):
    f32, bf16 = jnp.float32, jnp.bfloat16
    any_ = pl.BlockSpec(memory_space=pltpu.HBM)
    vm = pl.BlockSpec(memory_space=pltpu.VMEM)
    own = pl.pallas_call(
        pack_kernel,
        out_shape=jax.ShapeDtypeStruct((ROWS, 2 * HD), bf16),
        in_specs=[any_, any_, any_],
        out_specs=vm,
        scratch_shapes=[pltpu.VMEM((1, TOK), jnp.int32), pltpu.SemaphoreType.DMA((3,))],
        name="pack",
        cost_estimate=pl.CostEstimate(flops=4 << 30, bytes_accessed=16 << 20, transcendentals=0),
    )(keys, values, positions.reshape(1, TOK))
    swap = lambda a: lax.ppermute(a, "c", SWAP)

    def hop(a, shift):
        return lax.ppermute(a, "z", ring(shift))

    u1 = hop(own, 1)
    d1 = hop(own, -1)
    x4 = hop(own, 4)
    u2 = hop(u1, 1)
    d2 = hop(d1, -1)
    u3 = hop(u2, 1)
    d3 = hop(d2, -1)

    heads = lambda w, t: jax.ShapeDtypeStruct((8, TOK, w), t)
    state = jax.ShapeDtypeStruct((2 * HD, 2 * HD), f32)
    qf, m, accl, stu = call(
        local_kernel,
        (
            heads(256, bf16),
            heads(HD, f32),
            heads(256, f32),
            heads(256, f32),
        ),
        flops=8 * 2 * 256 * 128 * 1500,
        nbytes=8 << 20,
    )(own, queries, query_map, key_map)
    arrivals = [swap(own)]
    for a in (u1, d1, x4, u2, d2):
        arrivals += [a, swap(a)]
    m, accl, st = call(
        mid_kernel,
        (heads(HD, f32), heads(256, f32), state),
        flops=8 * 2 * 256 * 128 * 6000,
        nbytes=8 << 20,
    )(*arrivals, queries, key_map, m, accl)
    tail = [u3, swap(u3), d3, swap(d3)]
    return call(
        last_kernel,
        jax.ShapeDtypeStruct((TOK, 8 * HD), bf16),
        scratch=(
            pltpu.VMEM((8, TOK, HD), f32),
            pltpu.VMEM((8, TOK, 256), f32),
            pltpu.VMEM((2 * HD, 2 * HD), f32),
        ),
        flops=8 * 2 * 256 * 128 * 3000,
        nbytes=8 << 20,
    )(*tail, queries, key_map, qf, stu, m, accl, st)


def solution(mesh):
    split = Mesh(mesh.devices.reshape(8, 2, mesh.shape["head"]), ("z", "c", "head"))
    seq = ("z", "c")
    placed = (P(seq, "head"), P(seq, None), P(seq, None), P("head", None, None), P(), P(seq))
    return jax.shard_map(
        per_device, mesh=split, in_specs=placed, out_specs=P(seq, "head"), check_vma=False
    )
```

time: 45.7 us -> 41.3 us (0.904)
  local copies, waits for them, and re-layouts: 3.85 us -> 0.91 us
  Pallas kernels: 22.4 us -> 19.8 us
  starting transfers between devices: 16.7 us -> 18.1 us
    unnamed x12 -> x8, local copies, waits for them, and re-layouts: 3.85 us -> 0.91 us
    pallas_call x1, Pallas kernels: 11.1 us -> 9.41 us  [per_device(): call(mid_kernel, (heads(HD, f32), heads(256, f32), state), flops=8 * 2 *...]
    ppermute x8, starting transfers between devices: 6.77 us -> 8.08 us  [per_device(): swap = lambda a: lax.ppermute(a, 'c', SWAP)]
    pallas_call x1, Pallas kernels: 2.3 us -> 1.66 us  [per_device(): pl.pallas_call(pack_kernel, out_shape=jax.ShapeDtypeStruct((ROWS, 2 * HD)...]
where the time goes in v2:
time: 41.3 us; the launch traced here: 41.2 us
  Pallas kernels  19.8 us (48%)
  starting transfers between devices  18.1 us (44%)
  waiting for transfers between devices  2.41 us (6%)
  local copies, waits for them, and re-layouts  0.91 us (2%)
    ppermute x7, starting transfers between devices, hop(): return lax.ppermute(a, 'z', ring(shift))  9.98 us
    pallas_call x1, Pallas kernels, per_device(): call(mid_kernel, (heads(HD, f32), heads(256, f32), state), flops=8 * 2 *...  9.41 us
    ppermute x8, starting transfers between devices, per_device(): swap = lambda a: lax.ppermute(a, 'c', SWAP)  8.08 us
    pallas_call x1, Pallas kernels, per_device(): call(last_kernel, jax.ShapeDtypeStruct((TOK, 8 * HD), bf16), scratch=(plt...  5.51 us
    pallas_call x1, Pallas kernels, per_device(): call(local_kernel, (heads(256, bf16), heads(HD, f32), heads(256, f32), he...  3.17 us
    ppermute x7, waiting for transfers between devices, hop(): return lax.ppermute(a, 'z', ring(shift))  2.39 us
    pallas_call x1, Pallas kernels, per_device(): pl.pallas_call(pack_kernel, out_shape=jax.ShapeDtypeStruct((ROWS, 2 * HD)...  1.66 us
    unnamed x8, local copies, waits for them, and re-layouts  0.91 us
  transfers between devices with their start and end apart: 15, of which 1 were waited for; matrix products, arithmetic and copies ran while one was open for 0% of the time, Pallas kernels for 31%

profile of v2, /device:TPU:235, one launch (start us, length us, event | category | flops | bytes accessed | tf_op | source)
XLA Modules:
  0.0 41.2 jit_solution(12651659287578075879)
XLA Ops:
  0.0 0.0 copy-start
  0.0 0.0 copy-start.1
  0.0 0.0 copy-start.2
  0.0 1.7 %pack.1.own_ref = bf16[272,256]{1,0:T(8,128)(2,1)} custom-call(bf16[256,1024]{1,0:T(8,128)(2,1)} %keys_ref.1, bf16[256,1024]{1,0:T(8,128)(2,1)} %values_ref.1, s32[1,256]{1,0:T(1,128)} %bitcast.1), custom_call_target="tpu_custom_call" | custom-call | flops 4294967296 | bytes 16777216 | tf_op jit(solution)/shard_map/pack/pallas_call | solution.py:212
  1.7 0.1 collective-permute-start
  1.8 1.5 %collective-permute-start.4 = (bf16[272,256]{1,0:T(8,128)(2,1)}, bf16[272,256]{1,0:T(8,128)(2,1)S(1)}, u32[]{:S(2)}, u32[]{:S(2)}) collective-permute-start(bf16[272,256]{1,0:T(8,128)(2,1)} %pack.1.own_ref), channel_id=1, source_target_pairs={{0,224},{32,0},{64,32},{96,64},{128,96},{160,128},{192,160},{224,1... | collective-permute-start | bytes 417800 | tf_op jit(solution)/shard_map/ppermute | solution.py:224
  3.2 2.5 %collective-permute-start.11 = (bf16[272,256]{1,0:T(8,128)(2,1)}, bf16[272,256]{1,0:T(8,128)(2,1)S(1)}, u32[]{:S(2)}, u32[]{:S(2)}) collective-permute-start(bf16[272,256]{1,0:T(8,128)(2,1)} %pack.1.own_ref), channel_id=1, source_target_pairs={{0,128},{32,160},{64,192},{96,224},{128,0},{160,32},{192,64},{224,... | collective-permute-start | bytes 417800 | tf_op jit(solution)/shard_map/ppermute | solution.py:224
  5.8 1.2 %collective-permute-start.8 = (bf16[272,256]{1,0:T(8,128)(2,1)}, bf16[272,256]{1,0:T(8,128)(2,1)S(1)}, u32[]{:S(2)}, u32[]{:S(2)}) collective-permute-start(bf16[272,256]{1,0:T(8,128)(2,1)} %pack.1.own_ref), channel_id=1, source_target_pairs={{0,16},{16,0},{1,17},{17,1},{2,18},{18,2},{3,19},{19,3},{4,20},{20... | collective-permute-start | bytes 417800 | tf_op jit(solution)/shard_map/ppermute | solution.py:221
  7.0 0.0 collective-permute-done.u1
  7.0 3.0 %collective-permute-start.1 = (bf16[272,256]{1,0:T(8,128)(2,1)S(1)}, bf16[272,256]{1,0:T(8,128)(2,1)S(1)}, u32[]{:S(2)}, u32[]{:S(2)}) collective-permute-start(bf16[272,256]{1,0:T(8,128)(2,1)S(1)} %collective-permute-done.u1), channel_id=1, source_target_pairs={{0,32},{32,64},{64,96},{96,128},{128,160},{160,192},{192,224},{224... | collective-permute-start | bytes 417800 | tf_op jit(solution)/shard_map/ppermute | solution.py:224
  10.0 0.0 collective-permute-done.4.d1
  10.0 0.0 collective-permute-start.5
  10.0 1.2 %collective-permute-start.10 = (bf16[272,256]{1,0:T(8,128)(2,1)S(1)}, bf16[272,256]{1,0:T(8,128)(2,1)S(1)}, u32[]{:S(2)}, u32[]{:S(2)}) collective-permute-start(bf16[272,256]{1,0:T(8,128)(2,1)S(1)} %collective-permute-done.4.d1), channel_id=1, source_target_pairs={{0,16},{16,0},{1,17},{17,1},{2,18},{18,2},{3,19},{19,3},{4,20},{20... | collective-permute-start | bytes 417800 | tf_op jit(solution)/shard_map/ppermute | solution.py:221
  11.2 2.4 %collective-permute-done.11.x = bf16[272,256]{1,0:T(8,128)(2,1)S(1)} collective-permute-done((bf16[272,256]{1,0:T(8,128)(2,1)}, bf16[272,256]{1,0:T(8,128)(2,1)S(1)}, u32[]{:S(2)}, u32[]{:S(2)}) %collective-permute-start.11) | collective-permute-done | bytes 139296 | tf_op jit(solution)/shard_map/ppermute | solution.py:224
  13.6 2.4 %collective-permute-start.9 = (bf16[272,256]{1,0:T(8,128)(2,1)S(1)}, bf16[272,256]{1,0:T(8,128)(2,1)S(1)}, u32[]{:S(2)}, u32[]{:S(2)}) collective-permute-start(bf16[272,256]{1,0:T(8,128)(2,1)S(1)} %collective-permute-done.u1), channel_id=1, source_target_pairs={{0,16},{16,0},{1,17},{17,1},{2,18},{18,2},{3,19},{19,3},{4,20},{20... | collective-permute-start | bytes 417800 | tf_op jit(solution)/shard_map/ppermute | solution.py:221
  16.0 0.0 collective-permute-done.8.pb
  16.0 0.0 collective-permute-start.12
  16.0 0.0 collective-permute-done.1.u2
  16.0 2.9 %collective-permute-start.2 = (bf16[272,256]{1,0:T(8,128)(2,1)S(1)}, bf16[272,256]{1,0:T(8,128)(2,1)S(1)}, u32[]{:S(2)}, u32[]{:S(2)}) collective-permute-start(bf16[272,256]{1,0:T(8,128)(2,1)S(1)} %collective-permute-done.1.u2), channel_id=1, source_target_pairs={{0,32},{32,64},{64,96},{96,128},{128,160},{160,192},{192,224},{224... | collective-permute-start | bytes 417800 | tf_op jit(solution)/shard_map/ppermute | solution.py:224
  19.0 0.0 collective-permute-done.5.d2
  19.0 0.0 collective-permute-start.6
  19.0 0.0 collective-permute-done.10.d1s
  19.0 1.0 %collective-permute-start.13 = (bf16[272,256]{1,0:T(8,128)(2,1)S(1)}, bf16[272,256]{1,0:T(8,128)(2,1)S(1)}, u32[]{:S(2)}, u32[]{:S(2)}) collective-permute-start(bf16[272,256]{1,0:T(8,128)(2,1)S(1)} %collective-permute-done.1.u2), channel_id=1, source_target_pairs={{0,16},{16,0},{1,17},{17,1},{2,18},{18,2},{3,19},{19,3},{4,20},{20... | collective-permute-start | bytes 417800 | tf_op jit(solution)/shard_map/ppermute | solution.py:221
  19.9 0.0 collective-permute-done.9.u1s
  20.0 0.1 collective-permute-start.14
  20.1 0.0 copy-done
  20.1 0.0 copy-done.1
  20.1 0.0 copy-done.2
  20.1 0.0 copy-start.3
  20.1 0.9 %copy-done.3 = bf16[272,256]{1,0:T(8,128)(2,1)S(1)} copy-done((bf16[272,256]{1,0:T(8,128)(2,1)S(1)}, bf16[272,256]{1,0:T(8,128)(2,1)}, u32[]{:S(2)}) %copy-start.3) | copy-done | bytes 139288
  21.0 3.2 %shard_map.64 = (bf16[8,256,256]{2,1,0:T(8,128)(2,1)S(1)}, f32[8,256,128]{2,1,0:T(8,128)S(1)}, f32[8,256,256]{2,1,0:T(8,128)S(1)}, f32[8,256,256]{2,1,0:T(8,128)S(1)}) custom-call(bf16[272,256]{1,0:T(8,128)(2,1)S(1)} %copy-done.3, bf16[256,1024]{1,0:T(8,128)(2,1)S(1)} %copy-done, bf16[8,128,128]{2,1,0:T(8,128)(2,1)S(1)} %copy-done.2, ...), custom_call_target="tpu_custom_call" | custom-call | flops 786432000 | bytes 8388608 | tf_op jit(solution)/shard_map/pallas_call | solution.py:236
  24.2 0.0 collective-permute-done.2.u3
  24.2 0.5 %collective-permute-start.3 = (bf16[272,256]{1,0:T(8,128)(2,1)S(1)}, bf16[272,256]{1,0:T(8,128)(2,1)S(1)}, u32[]{:S(2)}, u32[]{:S(2)}) collective-permute-start(bf16[272,256]{1,0:T(8,128)(2,1)S(1)} %collective-permute-done.2.u3), channel_id=1, source_target_pairs={{0,16},{16,0},{1,17},{17,1},{2,18},{18,2},{3,19},{19,3},{4,20},{20... | collective-permute-start | bytes 417800 | tf_op jit(solution)/shard_map/ppermute | solution.py:221
  24.7 0.0 collective-permute-done.6.d3
  24.7 1.6 %collective-permute-start.7 = (bf16[272,256]{1,0:T(8,128)(2,1)S(1)}, bf16[272,256]{1,0:T(8,128)(2,1)S(1)}, u32[]{:S(2)}, u32[]{:S(2)}) collective-permute-start(bf16[272,256]{1,0:T(8,128)(2,1)S(1)} %collective-permute-done.6.d3), channel_id=1, source_target_pairs={{0,16},{16,0},{1,17},{17,1},{2,18},{18,2},{3,19},{19,3},{4,20},{20... | collective-permute-start | bytes 417800 | tf_op jit(solution)/shard_map/ppermute | solution.py:221
  26.3 0.0 collective-permute-done.12.xs
  26.3 0.0 collective-permute-done.13.u2s
  26.3 0.0 collective-permute-done.14.d2s
  26.3 9.4 %shard_map.65 = (f32[8,256,128]{2,1,0:T(8,128)S(1)}, f32[8,256,256]{2,1,0:T(8,128)S(1)}, f32[256,256]{1,0:T(8,128)S(1)}) custom-call(bf16[272,256]{1,0:T(8,128)(2,1)S(1)} %collective-permute-done.8.pb, bf16[272,256]{1,0:T(8,128)(2,1)S(1)} %collective-permute-done.u1, bf16[272,256]{1,0:T(8,128)(2,1)S(1)} %collective-permute-done.9.u1s, ...), custom_call_target="tpu_custom_call" | custom-call | flops 3145728000 | bytes 8388608 | tf_op jit(solution)/shard_map/pallas_call | solution.py:250
  35.7 0.0 collective-permute-done.3.u3s
  35.7 0.0 collective-permute-done.7.d3s
  35.7 5.5 %shard_map.66 = bf16[256,1024]{1,0:T(8,128)(2,1)} custom-call(bf16[272,256]{1,0:T(8,128)(2,1)S(1)} %collective-permute-done.2.u3, bf16[272,256]{1,0:T(8,128)(2,1)S(1)} %collective-permute-done.3.u3s, bf16[272,256]{1,0:T(8,128)(2,1)S(1)} %collective-permute-done.6.d3, bf16[272,256]{1,0:T(8,128)(2,1)S(1)} %collective-permute-done.7.d3s, ...), custom_call_target="tpu_custom_call" | custom-call | flops 1572864000 | bytes 8388608 | tf_op jit(solution)/shard_map/pallas_call | solution.py:257
Async XLA Ops:
  0.0 20.1 %copy-start = (bf16[256,1024]{1,0:T(8,128)(2,1)S(1)}, bf16[256,1024]{1,0:T(8,128)(2,1)}, u32[]{:S(2)}) copy-start(bf16[256,1024]{1,0:T(8,128)(2,1)} %q_ref.5) | copy-start | bytes 1572868
  0.0 20.1 %copy-start.1 = (bf16[8,128,128]{2,1,0:T(8,128)(2,1)S(1)}, bf16[8,128,128]{2,1,0:T(8,128)(2,1)}, u32[]{:S(2)}) copy-start(bf16[8,128,128]{2,1,0:T(8,128)(2,1)} %kmap_ref.5) | copy-start | bytes 786436
  0.0 20.1 %copy-start.2 = (bf16[8,128,128]{2,1,0:T(8,128)(2,1)S(1)}, bf16[8,128,128]{2,1,0:T(8,128)(2,1)}, u32[]{:S(2)}) copy-start(bf16[8,128,128]{2,1,0:T(8,128)(2,1)} %qmap_ref.1) | copy-start | bytes 786436
  1.7 5.3 %collective-permute-start = (bf16[272,256]{1,0:T(8,128)(2,1)}, bf16[272,256]{1,0:T(8,128)(2,1)S(1)}, u32[]{:S(2)}, u32[]{:S(2)}) collective-permute-start(bf16[272,256]{1,0:T(8,128)(2,1)} %pack.1.own_ref), channel_id=1, source_target_pairs={{0,32},{32,64},{64,96},{96,128},{128,160},{160,192},{192,224},{224... | collective-permute-start | bytes 417800 | tf_op jit(solution)/shard_map/ppermute | solution.py:224
  1.8 8.2 %collective-permute-start.4 = (bf16[272,256]{1,0:T(8,128)(2,1)}, bf16[272,256]{1,0:T(8,128)(2,1)S(1)}, u32[]{:S(2)}, u32[]{:S(2)}) collective-permute-start(bf16[272,256]{1,0:T(8,128)(2,1)} %pack.1.own_ref), channel_id=1, source_target_pairs={{0,224},{32,0},{64,32},{96,64},{128,96},{160,128},{192,160},{224,1... | collective-permute-start | bytes 417800 | tf_op jit(solution)/shard_map/ppermute | solution.py:224
  3.2 10.4 %collective-permute-start.11 = (bf16[272,256]{1,0:T(8,128)(2,1)}, bf16[272,256]{1,0:T(8,128)(2,1)S(1)}, u32[]{:S(2)}, u32[]{:S(2)}) collective-permute-start(bf16[272,256]{1,0:T(8,128)(2,1)} %pack.1.own_ref), channel_id=1, source_target_pairs={{0,128},{32,160},{64,192},{96,224},{128,0},{160,32},{192,64},{224,... | collective-permute-start | bytes 417800 | tf_op jit(solution)/shard_map/ppermute | solution.py:224
  5.8 10.2 %collective-permute-start.8 = (bf16[272,256]{1,0:T(8,128)(2,1)}, bf16[272,256]{1,0:T(8,128)(2,1)S(1)}, u32[]{:S(2)}, u32[]{:S(2)}) collective-permute-start(bf16[272,256]{1,0:T(8,128)(2,1)} %pack.1.own_ref), channel_id=1, source_target_pairs={{0,16},{16,0},{1,17},{17,1},{2,18},{18,2},{3,19},{19,3},{4,20},{20... | collective-permute-start | bytes 417800 | tf_op jit(solution)/shard_map/ppermute | solution.py:221
  7.0 9.0 %collective-permute-start.1 = (bf16[272,256]{1,0:T(8,128)(2,1)S(1)}, bf16[272,256]{1,0:T(8,128)(2,1)S(1)}, u32[]{:S(2)}, u32[]{:S(2)}) collective-permute-start(bf16[272,256]{1,0:T(8,128)(2,1)S(1)} %collective-permute-done.u1), channel_id=1, source_target_pairs={{0,32},{32,64},{64,96},{96,128},{128,160},{160,192},{192,224},{224... | collective-permute-start | bytes 417800 | tf_op jit(solution)/shard_map/ppermute | solution.py:224
  10.0 9.0 %collective-permute-start.5 = (bf16[272,256]{1,0:T(8,128)(2,1)S(1)}, bf16[272,256]{1,0:T(8,128)(2,1)S(1)}, u32[]{:S(2)}, u32[]{:S(2)}) collective-permute-start(bf16[272,256]{1,0:T(8,128)(2,1)S(1)} %collective-permute-done.4.d1), channel_id=1, source_target_pairs={{0,224},{32,0},{64,32},{96,64},{128,96},{160,128},{192,160},{224,1... | collective-permute-start | bytes 417800 | tf_op jit(solution)/shard_map/ppermute | solution.py:224
  10.0 9.0 %collective-permute-start.10 = (bf16[272,256]{1,0:T(8,128)(2,1)S(1)}, bf16[272,256]{1,0:T(8,128)(2,1)S(1)}, u32[]{:S(2)}, u32[]{:S(2)}) collective-permute-start(bf16[272,256]{1,0:T(8,128)(2,1)S(1)} %collective-permute-done.4.d1), channel_id=1, source_target_pairs={{0,16},{16,0},{1,17},{17,1},{2,18},{18,2},{3,19},{19,3},{4,20},{20... | collective-permute-start | bytes 417800 | tf_op jit(solution)/shard_map/ppermute | solution.py:221
  13.6 6.4 %collective-permute-start.9 = (bf16[272,256]{1,0:T(8,128)(2,1)S(1)}, bf16[272,256]{1,0:T(8,128)(2,1)S(1)}, u32[]{:S(2)}, u32[]{:S(2)}) collective-permute-start(bf16[272,256]{1,0:T(8,128)(2,1)S(1)} %collective-permute-done.u1), channel_id=1, source_target_pairs={{0,16},{16,0},{1,17},{17,1},{2,18},{18,2},{3,19},{19,3},{4,20},{20... | collective-permute-start | bytes 417800 | tf_op jit(solution)/shard_map/ppermute | solution.py:221
  16.0 10.3 %collective-permute-start.12 = (bf16[272,256]{1,0:T(8,128)(2,1)S(1)}, bf16[272,256]{1,0:T(8,128)(2,1)S(1)}, u32[]{:S(2)}, u32[]{:S(2)}) collective-permute-start(bf16[272,256]{1,0:T(8,128)(2,1)S(1)} %collective-permute-done.11.x), channel_id=1, source_target_pairs={{0,16},{16,0},{1,17},{17,1},{2,18},{18,2},{3,19},{19,3},{4,20},{20... | collective-permute-start | bytes 417800 | tf_op jit(solution)/shard_map/ppermute | solution.py:221
  16.0 8.1 %collective-permute-start.2 = (bf16[272,256]{1,0:T(8,128)(2,1)S(1)}, bf16[272,256]{1,0:T(8,128)(2,1)S(1)}, u32[]{:S(2)}, u32[]{:S(2)}) collective-permute-start(bf16[272,256]{1,0:T(8,128)(2,1)S(1)} %collective-permute-done.1.u2), channel_id=1, source_target_pairs={{0,32},{32,64},{64,96},{96,128},{128,160},{160,192},{192,224},{224... | collective-permute-start | bytes 417800 | tf_op jit(solution)/shard_map/ppermute | solution.py:224
  19.0 5.7 %collective-permute-start.6 = (bf16[272,256]{1,0:T(8,128)(2,1)S(1)}, bf16[272,256]{1,0:T(8,128)(2,1)S(1)}, u32[]{:S(2)}, u32[]{:S(2)}) collective-permute-start(bf16[272,256]{1,0:T(8,128)(2,1)S(1)} %collective-permute-done.5.d2), channel_id=1, source_target_pairs={{0,224},{32,0},{64,32},{96,64},{128,96},{160,128},{192,160},{224,1... | collective-permute-start | bytes 417800 | tf_op jit(solution)/shard_map/ppermute | solution.py:224
  19.0 7.3 %collective-permute-start.13 = (bf16[272,256]{1,0:T(8,128)(2,1)S(1)}, bf16[272,256]{1,0:T(8,128)(2,1)S(1)}, u32[]{:S(2)}, u32[]{:S(2)}) collective-permute-start(bf16[272,256]{1,0:T(8,128)(2,1)S(1)} %collective-permute-done.1.u2), channel_id=1, source_target_pairs={{0,16},{16,0},{1,17},{17,1},{2,18},{18,2},{3,19},{19,3},{4,20},{20... | collective-permute-start | bytes 417800 | tf_op jit(solution)/shard_map/ppermute | solution.py:221
  20.0 6.3 %collective-permute-start.14 = (bf16[272,256]{1,0:T(8,128)(2,1)S(1)}, bf16[272,256]{1,0:T(8,128)(2,1)S(1)}, u32[]{:S(2)}, u32[]{:S(2)}) collective-permute-start(bf16[272,256]{1,0:T(8,128)(2,1)S(1)} %collective-permute-done.5.d2), channel_id=1, source_target_pairs={{0,16},{16,0},{1,17},{17,1},{2,18},{18,2},{3,19},{19,3},{4,20},{20... | collective-permute-start | bytes 417800 | tf_op jit(solution)/shard_map/ppermute | solution.py:221
  20.1 0.9 %copy-start.3 = (bf16[272,256]{1,0:T(8,128)(2,1)S(1)}, bf16[272,256]{1,0:T(8,128)(2,1)}, u32[]{:S(2)}) copy-start(bf16[272,256]{1,0:T(8,128)(2,1)} %pack.1.own_ref) | copy-start | bytes 417796
  24.2 11.5 %collective-permute-start.3 = (bf16[272,256]{1,0:T(8,128)(2,1)S(1)}, bf16[272,256]{1,0:T(8,128)(2,1)S(1)}, u32[]{:S(2)}, u32[]{:S(2)}) collective-permute-start(bf16[272,256]{1,0:T(8,128)(2,1)S(1)} %collective-permute-done.2.u3), channel_id=1, source_target_pairs={{0,16},{16,0},{1,17},{17,1},{2,18},{18,2},{3,19},{19,3},{4,20},{20... | collective-permute-start | bytes 417800 | tf_op jit(solution)/shard_map/ppermute | solution.py:221
  24.7 11.0 %collective-permute-start.7 = (bf16[272,256]{1,0:T(8,128)(2,1)S(1)}, bf16[272,256]{1,0:T(8,128)(2,1)S(1)}, u32[]{:S(2)}, u32[]{:S(2)}) collective-permute-start(bf16[272,256]{1,0:T(8,128)(2,1)S(1)} %collective-permute-done.6.d3), channel_id=1, source_target_pairs={{0,16},{16,0},{1,17},{17,1},{2,18},{18,2},{3,19},{19,3},{4,20},{20... | collective-permute-start | bytes 417800 | tf_op jit(solution)/shard_map/ppermute | solution.py:221
